TPU v7x, 512 devices: a whole 4x8x8 slice. The times are simulated.
512 devices in a mesh: row: 16 (over y, core), col: 32 (over z, x).
Axes of the slice: x: 4, y: 8, z: 8, core: 2. Of those that a mesh axis runs over, the one named last changes fastest.
Arguments:
- matrix: float32 [4, 16, 256, 2, 32, 256], P(None, 'row', None, None, 'col'), as said below
- vectors: float32 [4, 16, 256, 256], P(None, 'row'), may hold values from -0.046875 to 0.046875
- t_factor: float32 [256, 256], replicated, as said below
Outputs:
- updated: float32 [4, 16, 256, 2, 32, 256], P(None, 'row', None, None, 'col')
Inputs may be any that keep to these rules, and one draw needn't show every extreme that they name: matrix is exactly symmetric as an 16384 x 16384 matrix: entry (i, j) equals entry (j, i). t_factor is upper triangular with its diagonal between 0.5 and 1.5.
All inputs are finite; a program needn't handle non-finite values.
Results may differ from a plain program's by a relative error of at most 0.000068.
Values sent between devices are 32-bit elements; how exact they have to be, the bound alone decides.
A program may use at most 64 MiB of HBM per device.

v0:
```python
import jax
import jax.numpy as jnp
from jax import lax
from jax.sharding import PartitionSpec as P


def spread(value, axis, root):
    mine = lax.axis_index(axis) == root
    return lax.psum(jnp.where(mine, value, jnp.zeros_like(value)), axis)


def product(left, right):
    return jnp.dot(left, right, precision=lax.Precision.HIGHEST, preferred_element_type=jnp.float32)


def per_device(matrix, vectors, t_factor):
    block_rows = vectors.shape[0]
    block_size = vectors.shape[2]
    block_cols = matrix.shape[3]
    row_devs = lax.axis_size("row")
    col_devs = lax.axis_size("col")
    col_ratio = col_devs // row_devs
    row_pos = lax.axis_index("row")
    col_pos = lax.axis_index("col")
    top_block = vectors[0, 0]
    unit_top = jnp.tril(top_block, -1) + jnp.eye(block_size, dtype=jnp.float32)
    first_block = jnp.where(row_pos == 0, unit_top, top_block)
    blocks = jnp.concatenate([first_block[None], vectors[1:, 0]], axis=0)
    chosen_ids = col_ratio * jnp.arange(block_cols, dtype=jnp.int32) + col_pos // row_devs
    source_row = col_pos % row_devs
    chosen = jnp.take(blocks, chosen_ids, axis=0)
    col_vecs = spread(chosen, "row", source_row).reshape(block_cols * block_size, block_size)
    row_vecs = blocks.reshape(block_rows * block_size, block_size)
    local_tile = matrix.reshape(block_rows * block_size, block_cols * block_size)
    summed = lax.psum(product(local_tile, col_vecs), "col")
    applied = product(summed, t_factor)
    inner = lax.psum(product(row_vecs.T, applied), "row")
    middle = product(t_factor.T, inner)
    coupled_rows = applied - 0.5 * product(row_vecs, middle)
    coupled_blocks = jnp.take(
        coupled_rows.reshape(block_rows, block_size, block_size), chosen_ids, axis=0
    )
    coupled_cols = spread(coupled_blocks, "row", source_row).reshape(
        block_cols * block_size, block_size
    )
    result = local_tile - product(row_vecs, coupled_cols.T) - product(coupled_rows, col_vecs.T)
    return result.reshape(matrix.shape)


def solution(mesh):
    in_specs = (P(None, "row", None, None, "col", None), P(None, "row", None, None), P())
    out_specs = P(None, "row", None, None, "col", None)
    return jax.shard_map(
        per_device, mesh=mesh, in_specs=in_specs, out_specs=out_specs, check_vma=False
    )
```

profile of v0, /device:TPU:1, one launch (start us, length us, event | category | flops | bytes accessed | tf_op | source)
XLA Modules:
  0.0 565.3 jit_solution(9547505962765150211)
XLA Ops:
  6.5 0.0 copy-start
  6.5 0.0 all-reduce.5.cloned.1.call-start
  6.6 1.2 slice_bitcast_fusion
  7.8 1.1 bitcast_select_fusion
  8.9 0.0 copy-start.3
  8.9 0.1 pad_maximum_fusion
  9.0 1.4 gather_fusion
  10.4 1.9 select_select_fusion.1
  12.3 0.0 all-reduce.5.cloned.1.call-update
  12.3 0.0 all-reduce.7.cloned.1.call-start
  12.4 0.0 copy-done.3
  12.4 8.1 %reduce = f32[4,256,2,256]{3,2,1,0:T(2,128)} reduce(f32[4,1,256,2,1,256]{5,4,3,2,1,0:T(1,128)S(1)} %copy-done.3, f32[]{:T(128)} %constant.58), dimensions={1,4}, to_apply=%param.5.reduce_sub_computation | reduce | bytes 4194308 | tf_op args[0]
  20.5 1.8 copy.5
  22.2 111.7 %all-reduce.5.cloned.1.call-done = f32[512,256]{1,0:T(8,128)} async-done(((f32[512,256]{1,0:T(8,128)}), f32[512,256]{1,0:T(8,128)}) %all-reduce.5.cloned.1.call-update) | async-done | bytes 524304 | tf_op jit(solution)/shard_map/psum | solution.py:9
  133.9 5.5 convolution_bitcast_fusion
  139.4 0.0 all-reduce.7.cloned.1.call-update
  139.4 0.2 all-reduce.9.cloned.1.call-start
  139.7 158.1 %all-reduce.7.cloned.1.call-done = f32[1024,256]{0,1:T(8,128)} async-done(((f32[1024,256]{0,1:T(8,128)}), f32[1024,256]{0,1:T(8,128)}) %all-reduce.7.cloned.1.call-update) | async-done | bytes 1048592 | tf_op jit(solution)/shard_map/psum | solution.py:35
  297.7 0.0 copy-done
  297.7 3.0 fusion.2
  300.8 0.0 copy-start.1
  300.8 1.0 copy-done.1
  301.7 2.5 fusion.3
  304.3 0.0 all-reduce.9.cloned.1.call-update
  304.3 0.0 all-reduce.11.cloned.1.call-start
  304.3 116.9 %all-reduce.9.cloned.1.call-done = f32[256,256]{1,0:T(8,128)} async-done(((f32[256,256]{1,0:T(8,128)}), f32[256,256]{1,0:T(8,128)}) %all-reduce.9.cloned.1.call-update) | async-done | bytes 262160 | tf_op jit(solution)/shard_map/psum | solution.py:37
  421.3 1.5 fusion.4
  422.8 3.2 fusion
  426.0 2.6 gather_fusion.1
  428.6 1.9 select_select_fusion
  430.6 0.0 all-reduce.11.cloned.1.call-update
  430.6 117.0 %all-reduce.11.cloned.1.call-done = f32[512,256]{1,0:T(8,128)} async-done(((f32[512,256]{1,0:T(8,128)}), f32[512,256]{1,0:T(8,128)}) %all-reduce.11.cloned.1.call-update) | async-done | bytes 524304 | tf_op jit(solution)/shard_map/psum | solution.py:9
  547.6 0.0 copy-start.2
  547.6 0.0 copy-start.4
  547.6 3.0 fusion.5
  550.6 0.0 copy-done.2
  550.7 0.0 copy-done.4
  550.7 3.4 subtract_subtract_fusion
  554.1 4.7 reshape.111
  (4 shorter events, 0.0 us)
Async XLA Ops:
  6.5 291.2 %copy-start = (f32[256,256]{1,0:T(8,128)S(1)}, f32[256,256]{1,0:T(8,128)}, u32[]{:S(2)}) copy-start(f32[256,256]{1,0:T(8,128)} %param.7) | copy-start | bytes 786436
  6.5 127.4 %all-reduce.5.cloned.1.call-start = ((), (), s32[]{:S(2)}) async-start(), calls=%async_computation | async-start | bytes 1048576 | tf_op jit(solution)/shard_map/psum | solution.py:9
  8.9 3.5 copy-start.3
  12.3 285.4 %all-reduce.7.cloned.1.call-start = ((), (), s32[]{:S(2)}) async-start(), calls=%async_computation.1 | async-start | bytes 2097152 | tf_op jit(solution)/shard_map/psum | solution.py:35
  139.4 281.8 %all-reduce.9.cloned.1.call-start = ((), (), s32[]{:S(2)}) async-start(), calls=%async_computation.2 | async-start | bytes 524288 | tf_op jit(solution)/shard_map/psum | solution.py:37
  300.8 1.0 copy-start.1
  304.3 243.3 %all-reduce.11.cloned.1.call-start = ((), (), s32[]{:S(2)}) async-start(), calls=%async_computation.3 | async-start | bytes 1048576 | tf_op jit(solution)/shard_map/psum | solution.py:9
  547.6 3.0 copy-start.2
  547.6 3.0 copy-start.4
Sparse Core Ops, SparseCore 0:
  12.5 121.3 all-reduce.4
  139.6 158.1 all-reduce.6
  304.4 116.7 all-reduce.8
  430.7 116.8 all-reduce.10
where the time goes:
time: 566 us; the launch traced here: 565 us
  waiting for transfers between devices  504 us (89%)
  matrix products  22.3 us (4%)
  between operations  13.3 us (2%)
  other arithmetic  13.1 us (2%)
  local copies, waits for them, and re-layouts  12.6 us (2%)
    psum x2, waiting for transfers between devices, spread(): return lax.psum(jnp.where(mine, value, jnp.zeros_like(value)), axis)  229 us
    psum x1, waiting for transfers between devices, per_device(): summed = lax.psum(product(local_tile, col_vecs), 'col')  158 us
    psum x1, waiting for transfers between devices, per_device(): inner = lax.psum(product(row_vecs.T, applied), 'row')  117 us
    dot_general x7, matrix products, product(): jnp.dot(left, right, precision=lax.Precision.HIGHEST, preferred_element_t...  22.3 us
  transfers between devices with their start and end apart: 4, of which 4 were waited for; matrix products, arithmetic and copies ran while one was open for 2% of the time, Pallas kernels for 0%

commit v1 on v0

v1 whole, which is shorter than its diff:
```python
import jax
import jax.numpy as jnp
from jax import lax
from jax.experimental import pallas as pl
from jax.experimental.pallas import tpu as pltpu
from jax.sharding import PartitionSpec as P

F32 = jnp.float32
BF16 = jnp.bfloat16
MESH = pl.DeviceIdType.MESH
NN = (((1,), (0,)), ((), ()))
NT = (((1,), (1,)), ((), ()))
Y, Z, X = 8, 8, 4


def split(value):
    high = value.astype(BF16)
    return high, (value - high.astype(F32)).astype(BF16)


def dot3(left, right, dims):
    def dot(a, b):
        return lax.dot_general(a, b, dims, preferred_element_type=F32)

    return dot(left[0], right[0]) + (dot(left[0], right[1]) + dot(left[1], right[0]))


def unit_lower(block):
    i = lax.broadcasted_iota(jnp.int32, block.shape, 0)
    k = lax.broadcasted_iota(jnp.int32, block.shape, 1)
    return jnp.where(i > k, block, jnp.where(i == k, 1.0, 0.0).astype(F32))


def kernel(
    a_hbm, v_hbm, t_hbm, o_hbm,
    a_s, v_s, t_s, o_s, vth, vtl, uh, ul, qt, xbuf, rsrc, rs, pct, prt, vc,
    uch, ucl, gsrc, gz, gsum, gx, gt,
    ld_sem, out_sem, one_s, one_r, y_s, y_r, z_s, z_r, x_s, x_r, gx_s, gx_r,
):
    row = lax.axis_index("row")
    col = lax.axis_index("col")
    y, j = row // 2, row % 2
    z, x = col // X, col % X
    half, pos = col // 16, col % 16
    mine = 8 * j + y
    held = pos + 1 - 2 * (pos % 2)
    t_target = (pos, 16 * half + mine + 1 - 2 * (mine % 2))
    v_target = (2 * (held % 8) + held // 8, 16 * half + row)
    partner = (2 * y + 1 - j, col)

    def y_peer(d):
        return (2 * ((y + d) % Y) + j, col)

    def z_peer(d):
        return (row, X * ((z + d) % Z) + x)

    def x_peer(d):
        return (row, X * z + (x + d) % X)

    def rows(start, size, step=16):
        return pl.ds(pl.multiple_of(start, step), size)

    started = []

    def send(src, dst, ssem, rsem, target):
        copy = pltpu.make_async_remote_copy(
            src_ref=src, dst_ref=dst, send_sem=ssem, recv_sem=rsem,
            device_id={"row": target[0], "col": target[1]}, device_id_type=MESH,
        )
        copy.start()
        started.append(copy)
        return copy

    load_v = pltpu.make_async_copy(v_hbm, v_s, ld_sem.at[4])
    load_v.start()
    load_t = pltpu.make_async_copy(t_hbm, t_s, ld_sem.at[5])

    def load_a(lr):
        part = rows(lr * 1024, 1024, 1024)
        return pltpu.make_async_copy(a_hbm.at[part], a_s.at[part], ld_sem.at[lr])

    for lr in range(4):
        load_a(lr).start()
    load_t.start()

    barrier = pltpu.get_barrier_semaphore()
    greeted = (
        [y_peer(d) for d in range(1, Y)] + [z_peer(d) for d in range(1, Z)]
        + [x_peer(d) for d in range(1, X)] + [partner, t_target, v_target]
    )
    for peer in greeted:
        pl.semaphore_signal(
            barrier, inc=1, device_id={"row": peer[0], "col": peer[1]}, device_id_type=MESH
        )

    load_v.wait()

    @pl.loop(0, 4)
    def _(lr):
        block = v_s[lr]
        fixed = jnp.where(row * 4 + lr == 0, unit_lower(block), block)
        high, low = split(fixed.T)
        vth[lr] = high
        vtl[lr] = low
        high, low = split(fixed)
        uh[lr] = high
        ul[lr] = low

    qt[...] = jnp.zeros_like(qt)

    @pl.loop(0, 4)
    def _(lr):
        load_a(lr).wait()
        left = (vth[lr], vtl[lr])
        for lc in range(2):
            block = jnp.concatenate(
                [a_s[pl.ds(lr * 1024 + 2 * lc + q, 256, stride=4), :] for q in range(2)], axis=1
            )
            qt[:, 256 * lc : 256 * lc + 256] += dot3(left, split(block), NN)

    pl.semaphore_wait(barrier, len(greeted))

    swap = send(qt.at[rows(128 * (1 - j), 128)], xbuf, one_s.at[0], one_r.at[0], partner)
    v_move = send(
        v_s.at[half + 2 * (held // 8), rows(32 * (held % 8), 32)],
        vc.at[rows(32 * held, 32)], one_s.at[1], one_r.at[1], v_target,
    )
    load_t.wait()
    swap.wait_recv()
    rsrc[...] = qt[rows(128 * j, 128), :] + xbuf[...]
    order = (4, 3, 5, 2, 6, 1, 7)
    scatter = [
        send(
            rsrc.at[rows(16 * ((y + d) % Y), 16)], rs.at[d],
            y_s.at[0, d], y_r.at[0, d], y_peer(d),
        )
        for d in order
    ]
    factor = split(t_s[...])

    @pl.loop(0, 4)
    def _(lr):
        high, low = split(dot3((uh[lr], ul[lr]), factor, NT))
        uh[lr] = high
        ul[lr] = low

    v_move.wait_recv()
    v_part = vc.at[rows(32 * mine, 32)]
    v_gather = [
        send(v_part, v_part, y_s.at[1, d], y_r.at[1, d], y_peer(d)) for d in order
    ]
    total = rsrc[rows(16 * y, 16), :]
    for copy, d in zip(scatter, order):
        copy.wait_recv()
        total = total + rs[d]
    own = rows(16 * mine, 16)
    pct[own, :] = total
    t_move = send(
        pct.at[own], prt.at[half, own], one_s.at[2], one_r.at[2], t_target
    )
    p_gather = [
        send(pct.at[own], pct.at[own], y_s.at[2, d], y_r.at[2, d], y_peer(d)) for d in order
    ]
    for copy in v_gather:
        copy.wait_recv()
    v_half = vc.at[rows(256 * j, 256)]
    v_swap = send(v_half, v_half, one_s.at[3], one_r.at[3], partner)

    t_move.wait_recv()
    chunk = prt.at[half, rows(16 * held, 16)]
    z_gather = {
        d: send(chunk, chunk, z_s.at[0, d], z_r.at[0, d], z_peer(d)) for d in order
    }

    def chunk_of(zi, xi):
        p = 4 * (zi % 4) + xi
        return prt.at[zi // 4, rows(16 * (p + 1 - 2 * (p % 2)), 16)]

    def half_of(zi, xi, which):
        p = 4 * (zi % 4) + xi
        return prt.at[zi // 4, rows(16 * (p + 1 - 2 * (p % 2)) + 8 * which, 8, 8)]

    def x_send(d):
        part = chunk_of((z - d) % Z, x)
        return [
            send(part, part, x_s.at[side, d], x_r.at[side, d], x_peer(1 - 2 * side))
            for side in range(2)
        ]

    x_gather = {0: x_send(0)}

    v_swap.wait_recv()

    first = vc[0:256, :]
    first = jnp.where(col == 0, unit_lower(first), first)
    v_cols = split(jnp.concatenate([first, vc[256:512, :]], axis=0))
    gsrc[...] = dot3(split(total), v_cols, NN)
    g_z = [send(gsrc, gz.at[d], z_s.at[1, d], z_r.at[1, d], z_peer(d)) for d in order]

    for d in (1, 7, 2, 6, 3, 5, 4):
        z_gather[d].wait_recv()
        x_gather[d] = x_send(d)

    high, low = split(dot3(factor, v_cols, NT))
    uch[...] = high
    ucl[...] = low

    for copy in p_gather:
        copy.wait_recv()
    p_half = pct.at[rows(128 * j, 128)]
    p_swap = send(p_half, p_half, one_s.at[4], one_r.at[4], partner)

    part_sum = gsrc[...]
    for copy, d in zip(g_z, order):
        copy.wait_recv()
        part_sum = part_sum + gz[d]
    gsum[...] = part_sum
    g_x = [
        send(gsum, gx.at[d], gx_s.at[d], gx_r.at[d], x_peer(d)) for d in range(1, X)
    ]

    forward = []
    for d in (0, 1, 7, 2, 6, 3, 5, 4):
        for side in range(2):
            x_gather[d][side].wait_recv()
            part = half_of((z - d) % Z, (x - 1 + 2 * side) % X, side)
            forward.append(
                send(part, part, x_s.at[2 + side, d], x_r.at[2 + side, d], x_peer(1 - 2 * side))
            )

    part_sum = gsum[...]
    for d, copy in zip(range(1, X), g_x):
        copy.wait_recv()
        part_sum = part_sum + gx[d]
    gt[own, :] = part_sum
    g_gather = [
        send(gt.at[own], gt.at[own], y_s.at[3, d], y_r.at[3, d], y_peer(d)) for d in order
    ]

    for copy in forward:
        copy.wait_recv()

    @pl.loop(0, 4)
    def _(lr):
        h = lr % 2
        left = split(prt[h, :, pl.ds(pl.multiple_of(256 * (lr // 2), 256), 256)].T)
        for lc in range(2):
            cols = slice(256 * lc, 256 * lc + 256)
            delta = dot3(left, (uch[:, cols], ucl[:, cols]), NN)
            for q in range(2):
                where = pl.ds(lr * 1024 + 2 * lc + q, 256, stride=4)
                o_s[where, :] = a_s[where, :] - delta[:, 128 * q : 128 * q + 128]

    for copy in g_gather:
        copy.wait_recv()
    g_half = gt.at[rows(128 * j, 128)]
    g_swap = send(g_half, g_half, one_s.at[5], one_r.at[5], partner)
    p_swap.wait_recv()
    g_swap.wait_recv()
    coupled = split(pct[...] - dot3(split(gt[...]), (uch[...], ucl[...]), NN))
    uch[...] = coupled[0]
    ucl[...] = coupled[1]

    def store(lr):
        part = rows(lr * 1024, 1024, 1024)
        return pltpu.make_async_copy(o_s.at[part], o_hbm.at[part], out_sem.at[lr])

    @pl.loop(0, 4)
    def _(lr):
        left = (uh[lr], ul[lr])
        for lc in range(2):
            cols = slice(256 * lc, 256 * lc + 256)
            delta = dot3(left, (uch[:, cols], ucl[:, cols]), NN)
            for q in range(2):
                where = pl.ds(lr * 1024 + 2 * lc + q, 256, stride=4)
                o_s[where, :] = o_s[where, :] - delta[:, 128 * q : 128 * q + 128]
        store(lr).start()

    for copy in started:
        copy.wait_send()
    for lr in range(4):
        store(lr).wait()


def per_device(matrix, vectors, t_factor):
    a = matrix.reshape(4096, 128)
    v = vectors.reshape(4, 256, 256)
    vm = pltpu.VMEM
    dma = pltpu.SemaphoreType.DMA
    out = pl.pallas_call(
        kernel,
        out_shape=jax.ShapeDtypeStruct((4096, 128), F32),
        in_specs=[pl.BlockSpec(memory_space=pl.ANY)] * 3,
        out_specs=pl.BlockSpec(memory_space=pl.ANY),
        scratch_shapes=[
            vm((4096, 128), F32), vm((4, 256, 256), F32), vm((256, 256), F32),
            vm((4096, 128), F32),
            vm((4, 256, 256), BF16), vm((4, 256, 256), BF16),
            vm((4, 256, 256), BF16), vm((4, 256, 256), BF16),
            vm((256, 512), F32), vm((128, 512), F32), vm((128, 512), F32),
            vm((8, 16, 512), F32), vm((256, 512), F32), vm((2, 256, 512), F32),
            vm((512, 256), F32), vm((256, 512), BF16), vm((256, 512), BF16),
            vm((16, 256), F32), vm((8, 16, 256), F32), vm((16, 256), F32),
            vm((4, 16, 256), F32), vm((256, 256), F32),
            dma((6,)), dma((4,)), dma((6,)), dma((6,)), dma((4, 8)), dma((4, 8)),
            dma((2, 8)), dma((2, 8)), dma((4, 8)), dma((4, 8)), dma((4,)), dma((4,)),
        ],
        compiler_params=pltpu.CompilerParams(collective_id=0, has_side_effects=True),
        name="band_update",
    )(a, v, t_factor)
    return out.reshape(matrix.shape)


def solution(mesh):
    in_specs = (P(None, "row", None, None, "col", None), P(None, "row", None, None), P())
    out_specs = P(None, "row", None, None, "col", None)
    return jax.shard_map(
        per_device, mesh=mesh, in_specs=in_specs, out_specs=out_specs, check_vma=False
    )
```

time: 566 us -> 67.3 us (0.12)
  waiting for transfers between devices: 504 us -> 0 us
  Pallas kernels: 0 us -> 62.8 us
  matrix products: 22.3 us -> 0 us
  between operations: 13.3 us -> 0.01 us
  other arithmetic: 13.1 us -> 0 us
  local copies, waits for them, and re-layouts: 12.6 us -> 4.35 us
    psum x4 -> x0, waiting for transfers between devices: 504 us -> none  [the longest x2 229 us: spread(): return lax.psum(jnp.where(mine, value, jnp.zeros_like(value)), axis)]
    pallas_call x0 -> x1, Pallas kernels: none -> 62.8 us  [per_device(): pl.pallas_call(kernel, out_shape=jax.ShapeDtypeStruct((4096, 128), F32),...]
    dot_general x7 -> x0, matrix products: 22.3 us -> none  [product(): jnp.dot(left, right, precision=lax.Precision.HIGHEST, preferred_element_t...]
    unnamed x1 -> x0, other arithmetic: 8.06 us -> none
  transfers between devices with their start and end apart: 4 -> 0, of which waited for: 4 -> 0; matrix products, arithmetic and copies ran while one was open for 2% -> 0% of each run, Pallas kernels for 0% -> 0%
where the time goes in v1:
time: 67.3 us; the launch traced here: 67.2 us
  Pallas kernels  62.8 us (93%)
  local copies, waits for them, and re-layouts  4.35 us (6%)
    pallas_call x1, Pallas kernels, per_device(): pl.pallas_call(kernel, out_shape=jax.ShapeDtypeStruct((4096, 128), F32),...  62.8 us
    unnamed x1, local copies, waits for them, and re-layouts  4.35 us

profile of v1, /device:TPU:1, one launch (start us, length us, event | category | flops | bytes accessed | tf_op | source)
XLA Modules:
  0.0 67.2 jit_solution(4860607865492937416)
XLA Ops:
  0.0 62.8 %band_update.1 = f32[4096,128]{1,0:T(8,128)} custom-call(f32[4096,128]{1,0:T(8,128)} %bitcast.4, f32[4,256,256]{2,1,0:T(8,128)} %bitcast.5, f32[256,256]{1,0:T(8,128)} %t_hbm.1), custom_call_target="tpu_custom_call" | custom-call | tf_op jit(solution)/shard_map/band_update/pallas_call | solution.py:290
  62.8 4.3 %copy.6 = f32[4,1,256,2,1,256]{5,4,3,2,1,0:T(1,128)} copy(f32[4,1,256,2,1,256]{5,4,3,2,1,0:T(1,128)} %bitcast.3) | data formatting | bytes 4194304

commit v2 on v0

v2 whole, which is shorter than its diff:
```python
import jax
import jax.numpy as jnp
from jax import lax
from jax.experimental import pallas as pl
from jax.experimental.pallas import tpu as pltpu
from jax.sharding import PartitionSpec as P

F32 = jnp.float32
BF16 = jnp.bfloat16
MESH = pl.DeviceIdType.MESH
NN = (((1,), (0,)), ((), ()))
NT = (((1,), (1,)), ((), ()))
Y, Z, X = 8, 8, 4
VMEM_LIMIT = 24 * 1024 * 1024


def split(value):
    high = value.astype(BF16)
    return high, (value - high.astype(F32)).astype(BF16)


def dot3(left, right, dims):
    def dot(a, b):
        return lax.dot_general(a, b, dims, preferred_element_type=F32)

    return dot(left[0], right[0]) + (dot(left[0], right[1]) + dot(left[1], right[0]))


def unit_lower(block):
    i = lax.broadcasted_iota(jnp.int32, block.shape, 0)
    k = lax.broadcasted_iota(jnp.int32, block.shape, 1)
    return jnp.where(i > k, block, jnp.where(i == k, 1.0, 0.0).astype(F32))


def kernel(
    a_s, v_s, t_s, o_s, uh, ul, wh, wl,
    vth, vtl, qt, xbuf, rsrc, rs, pct, prt, vc, uch, ucl, gsrc, gz, gsum, gx, gt,
    one_s, one_r, v_s_s, v_s_r, rs_s, rs_r, y_s, y_r,
    z_s, z_r, gz_s, gz_r, x_s, x_r, f_s, f_r, gx_s, gx_r,
):
    row = lax.axis_index("row")
    col = lax.axis_index("col")
    y, j = row // 2, row % 2
    z, x = col // X, col % X
    half, pos = col // 16, col % 16

    def flip(index):
        return index + 1 - 2 * (index % 2)

    def slice_at(position):
        other = flip(position)
        return 8 * (other % 2) + other // 2

    mine, held = 8 * j + y, slice_at(pos)
    t_target, t_source = (pos, 16 * half + flip(row)), (flip(pos), 16 * half + row)
    partner = (2 * y + 1 - j, col)

    def y_peer(d):
        return (2 * ((y + d) % Y) + j, col)

    def z_peer(d):
        return (row, X * ((z + d) % Z) + x)

    def x_peer(d):
        return (row, X * z + (x + d) % X)

    def v_target(d):
        return (2 * ((held + d) % Y) + held // 8, 16 * half + row)

    def rows(start, size, step=16):
        return pl.ds(pl.multiple_of(start, step), size)

    started = []

    def send(src, dst, ssem, rsem, target):
        copy = pltpu.make_async_remote_copy(
            src_ref=src, dst_ref=dst, send_sem=ssem, recv_sem=rsem,
            device_id={"row": target[0], "col": target[1]}, device_id_type=MESH,
        )
        copy.start()
        started.append(copy)
        return copy

    barrier = pltpu.get_barrier_semaphore()
    greeted = (
        [y_peer(d) for d in range(1, Y)] + [z_peer(d) for d in range(1, Z)]
        + [x_peer(d) for d in range(1, X)] + [partner, t_source]
        + [(pos, 16 * half + 2 * i + 1 - j) for i in range(8)]
    )
    for peer in greeted:
        pl.semaphore_signal(
            barrier, inc=1, device_id={"row": peer[0], "col": peer[1]}, device_id_type=MESH
        )

    for lr in range(4):
        block = v_s[lr]
        if lr == 0:
            block = jnp.where(row == 0, unit_lower(block), block)
        high, low = split(block.T)
        vth[:, 256 * lr : 256 * lr + 256] = high
        vtl[:, 256 * lr : 256 * lr + 256] = low
        high, low = split(block)
        uh[lr] = high
        ul[lr] = low

    def partial(lc):
        block = jnp.concatenate(
            [a_s[pl.ds(2 * lc + q, 1024, stride=4), :] for q in range(2)], axis=1
        )
        qt[lc] = dot3((vth[...], vtl[...]), split(block), NN)

    def swap_of(lc):
        return send(
            qt.at[lc, rows(128 * (1 - j), 128)], xbuf.at[lc],
            one_s.at[lc], one_r.at[lc], partner,
        )

    order = (4, 3, 5, 2, 6, 1, 7)

    partial(0)
    pl.semaphore_wait(barrier, len(greeted))
    swaps = [swap_of(0)]
    v_part = v_s.at[half + 2 * (held // 8), rows(32 * (held % 8), 32)]
    v_moves = [
        send(v_part, vc.at[rows(32 * held, 32)], v_s_s.at[d], v_s_r.at[d], v_target(d))
        for d in range(8)
    ]
    partial(1)
    swaps.append(swap_of(1))
    scatter = []
    for lc in range(2):
        swaps[lc].wait_recv()
        rsrc[lc] = qt[lc, rows(128 * j, 128), :] + xbuf[lc]
        scatter.append([
            send(
                rsrc.at[lc, rows(16 * ((y + d) % Y), 16)], rs.at[lc, d],
                rs_s.at[lc, d], rs_r.at[lc, d], y_peer(d),
            )
            for d in order
        ])
    factor = split(t_s[...])
    for lr in range(4):
        high, low = split(dot3((uh[lr], ul[lr]), factor, NT))
        uh[lr] = high
        ul[lr] = low
    own = rows(16 * mine, 16)
    totals, t_moves = [], []
    for lc in range(2):
        total = rsrc[lc, rows(16 * y, 16), :]
        for copy, d in zip(scatter[lc], order):
            copy.wait_recv()
            total = total + rs[lc, d]
        pct[lc, own, :] = total
        totals.append(total)
        t_moves.append(send(
            pct.at[lc, own], prt.at[half, lc, own], one_s.at[2 + lc], one_r.at[2 + lc], t_target
        ))
    p_part = pct.at[:, own]
    p_gather = [
        send(p_part, p_part, y_s.at[0, d], y_r.at[0, d], y_peer(d)) for d in order
    ]
    for copy in v_moves:
        copy.wait_recv()
    v_half = vc.at[rows(256 * j, 256)]
    v_swap = send(v_half, v_half, one_s.at[4], one_r.at[4], partner)
    v_swap.wait_recv()
    first = vc[0:256, :]
    first = jnp.where(col == 0, unit_lower(first), first)
    v_cols = [split(first), split(vc[256:512, :])]
    gsrc[...] = dot3(split(totals[0]), v_cols[0], NN) + dot3(split(totals[1]), v_cols[1], NN)
    g_z = [send(gsrc, gz.at[d], gz_s.at[d], gz_r.at[d], z_peer(d)) for d in order]
    for lc in range(2):
        high, low = split(dot3(factor, v_cols[lc], NT))
        uch[:, 256 * lc : 256 * lc + 256] = high
        ucl[:, 256 * lc : 256 * lc + 256] = low

    def chunk_of(zi, xi, lc):
        return prt.at[zi // 4, lc, rows(16 * slice_at(4 * (zi % 4) + xi), 16)]

    def x_send(d, lc):
        part = chunk_of((z - d) % Z, x, lc)
        return [
            send(part, part, x_s.at[side, lc, d], x_r.at[side, lc, d], x_peer(1 - 2 * side))
            for side in range(2)
        ]

    z_gather, x_gather = [], [{}, {}]
    for lc in range(2):
        t_moves[lc].wait_recv()
        chunk = chunk_of(z, x, lc)
        z_gather.append({
            d: send(chunk, chunk, z_s.at[lc, d], z_r.at[lc, d], z_peer(d)) for d in order
        })
        x_gather[lc][0] = x_send(0, lc)
    near = (1, 7, 2, 6, 3, 5, 4)
    forward = [[], []]

    def pass_on(d, lc):
        x_gather[lc][d][lc].wait_recv()
        part = chunk_of((z - d) % Z, (x - 1 + 2 * lc) % X, lc)
        forward[lc].append(
            send(part, part, f_s.at[lc, d], f_r.at[lc, d], x_peer(1 - 2 * lc))
        )

    for d in near:
        z_gather[0][d].wait_recv()
        x_gather[0][d] = x_send(d, 0)
    for d in near:
        z_gather[1][d].wait_recv()
        x_gather[1][d] = x_send(d, 1)
    part_sum = gsrc[...]
    for copy, d in zip(g_z, order):
        copy.wait_recv()
        part_sum = part_sum + gz[d]
    gsum[...] = part_sum
    g_x = [
        send(gsum, gx.at[d], gx_s.at[d], gx_r.at[d], x_peer(d)) for d in range(1, X)
    ]
    for d in (0,) + near:
        pass_on(d, 0)
    for d in (0,) + near:
        pass_on(d, 1)
    for d, copy in zip(range(1, X), g_x):
        copy.wait_recv()
        part_sum = part_sum + gx[d]
    gt[own, :] = part_sum
    g_gather = [
        send(gt.at[own], gt.at[own], y_s.at[1, d], y_r.at[1, d], y_peer(d)) for d in order
    ]
    for copy in p_gather:
        copy.wait_recv()
    p_half = pct.at[:, rows(128 * j, 128)]
    p_swap = send(p_half, p_half, one_s.at[5], one_r.at[5], partner)

    for lc in range(2):
        for d in (0,) + near:
            x_gather[lc][d][1 - lc].wait_recv()
        for copy in forward[lc]:
            copy.wait_recv()
        for h in range(2):
            lr = h + 2 * lc
            left = split(prt[h, lc].T)
            for oc in range(2):
                cols = slice(256 * oc, 256 * oc + 256)
                delta = dot3(left, (uch[:, cols], ucl[:, cols]), NN)
                for q in range(2):
                    where = pl.ds(lr * 1024 + 2 * oc + q, 256, stride=4)
                    o_s[where, :] = a_s[where, :] - delta[:, 128 * q : 128 * q + 128]
    for copy in g_gather:
        copy.wait_recv()
    g_half = gt.at[rows(128 * j, 128)]
    g_swap = send(g_half, g_half, one_s.at[6], one_r.at[6], partner)
    p_swap.wait_recv()
    g_swap.wait_recv()
    inner = split(gt[...])
    for lc in range(2):
        cols = slice(256 * lc, 256 * lc + 256)
        high, low = split(pct[lc] - dot3(inner, (uch[:, cols], ucl[:, cols]), NN))
        wh[:, cols] = high
        wl[:, cols] = low
    for copy in started:
        copy.wait_send()


def finish_kernel(o_ref, uh_ref, ul_ref, wh_ref, wl_ref, out_ref):
    left = (uh_ref[0], ul_ref[0])
    count = left[0].shape[0]
    for oc in range(2):
        cols = slice(256 * oc, 256 * oc + 256)
        delta = dot3(left, (wh_ref[:, cols], wl_ref[:, cols]), NN)
        for q in range(2):
            where = pl.ds(2 * oc + q, count, stride=4)
            out_ref[where, :] = o_ref[where, :] - delta[:, 128 * q : 128 * q + 128]


def per_device(matrix, vectors, t_factor):
    a = matrix.reshape(4096, 128)
    v = vectors.reshape(4, 256, 256)
    vm = pltpu.VMEM
    dma = pltpu.SemaphoreType.DMA
    shape = jax.ShapeDtypeStruct
    parts = pl.pallas_call(
        kernel,
        out_shape=[
            shape((4096, 128), F32), shape((4, 256, 256), BF16), shape((4, 256, 256), BF16),
            shape((256, 512), BF16), shape((256, 512), BF16),
        ],
        in_specs=[pl.BlockSpec(memory_space=pltpu.VMEM)] * 3,
        out_specs=[pl.BlockSpec(memory_space=pltpu.VMEM)] * 5,
        scratch_shapes=[
            vm((256, 1024), BF16), vm((256, 1024), BF16),
            vm((2, 256, 256), F32), vm((2, 128, 256), F32), vm((2, 128, 256), F32),
            vm((2, 8, 16, 256), F32), vm((2, 256, 256), F32), vm((2, 2, 256, 256), F32),
            vm((512, 256), F32), vm((256, 512), BF16), vm((256, 512), BF16),
            vm((16, 256), F32), vm((8, 16, 256), F32), vm((16, 256), F32),
            vm((4, 16, 256), F32), vm((256, 256), F32),
            dma((7,)), dma((7,)), dma((8,)), dma((8,)),
            dma((2, 8)), dma((2, 8)), dma((2, 8)), dma((2, 8)),
            dma((2, 8)), dma((2, 8)), dma((8,)), dma((8,)),
            dma((2, 2, 8)), dma((2, 2, 8)), dma((2, 8)), dma((2, 8)), dma((4,)), dma((4,)),
        ],
        compiler_params=pltpu.CompilerParams(
            collective_id=0, has_side_effects=True, vmem_limit_bytes=VMEM_LIMIT
        ),
        name="band_update",
    )(a, v, t_factor)
    steps = 8
    out = pl.pallas_call(
        finish_kernel,
        grid=(steps,),
        out_shape=shape((4096, 128), F32),
        in_specs=[
            pl.BlockSpec((4096 // steps, 128), lambda i: (i, 0)),
            pl.BlockSpec((1, 1024 // steps, 256), lambda i: (i // 2, i % 2, 0)),
            pl.BlockSpec((1, 1024 // steps, 256), lambda i: (i // 2, i % 2, 0)),
            pl.BlockSpec((256, 512), lambda i: (0, 0)),
            pl.BlockSpec((256, 512), lambda i: (0, 0)),
        ],
        out_specs=pl.BlockSpec((4096 // steps, 128), lambda i: (i, 0)),
        compiler_params=pltpu.CompilerParams(vmem_limit_bytes=VMEM_LIMIT // 2),
        name="band_finish",
    )(*parts)
    return out.reshape(matrix.shape)


def solution(mesh):
    in_specs = (P(None, "row", None, None, "col", None), P(None, "row", None, None), P())
    out_specs = P(None, "row", None, None, "col", None)
    return jax.shard_map(
        per_device, mesh=mesh, in_specs=in_specs, out_specs=out_specs, check_vma=False
    )
```

time: 566 us -> 66.9 us (0.12)
  waiting for transfers between devices: 504 us -> 0 us
  Pallas kernels: 0 us -> 62.9 us
  matrix products: 22.3 us -> 0 us
  between operations: 13.3 us -> 0.01 us
  other arithmetic: 13.1 us -> 0 us
  local copies, waits for them, and re-layouts: 12.6 us -> 3.76 us
    psum x4 -> x0, waiting for transfers between devices: 504 us -> none  [the longest x2 229 us: spread(): return lax.psum(jnp.where(mine, value, jnp.zeros_like(value)), axis)]
    pallas_call x0 -> x2, Pallas kernels: none -> 62.9 us  [the longest x1 58.7 us: per_device(): pl.pallas_call(kernel, out_shape=[shape((4096, 128), F32), shape((4, 256,...]
    dot_general x7 -> x0, matrix products: 22.3 us -> none  [product(): jnp.dot(left, right, precision=lax.Precision.HIGHEST, preferred_element_t...]
    unnamed x1 -> x0, other arithmetic: 8.06 us -> none
  transfers between devices with their start and end apart: 4 -> 0, of which waited for: 4 -> 0; matrix products, arithmetic and copies ran while one was open for 2% -> 0% of each run, Pallas kernels for 0% -> 0%
where the time goes in v2:
time: 66.9 us; the launch traced here: 66.7 us
  Pallas kernels  62.9 us (94%)
  local copies, waits for them, and re-layouts  3.76 us (6%)
    pallas_call x1, Pallas kernels, per_device(): pl.pallas_call(kernel, out_shape=[shape((4096, 128), F32), shape((4, 256,...  58.7 us
    pallas_call x1, Pallas kernels, per_device(): pl.pallas_call(finish_kernel, grid=(steps,), out_shape=shape((4096, 128),...  4.21 us
    unnamed x6, local copies, waits for them, and re-layouts  3.76 us

profile of v2, /device:TPU:1, one launch (start us, length us, event | category | flops | bytes accessed | tf_op | source)
XLA Modules:
  0.0 66.7 jit_solution(3938580763293050627)
XLA Ops:
  0.0 0.0 copy-start
  0.0 1.6 %copy-done = f32[4,1,256,2,1,256]{5,4,3,2,1,0:T(1,128)S(1)} copy-done((f32[4,1,256,2,1,256]{5,4,3,2,1,0:T(1,128)S(1)}, f32[4,1,256,2,1,256]{5,4,3,2,1,0:T(1,128)}, u32[]{:S(2)}) %copy-start) | copy-done | bytes 2097176
  1.6 0.0 copy-start.1
  1.6 1.2 %copy-done.1 = f32[4,1,256,256]{3,2,1,0:T(8,128)S(1)} copy-done((f32[4,1,256,256]{3,2,1,0:T(8,128)S(1)}, f32[4,1,256,256]{3,2,1,0:T(8,128)}, u32[]{:S(2)}) %copy-start.1) | copy-done | bytes 1048600
  2.8 0.0 copy-start.2
  2.8 0.9 %copy-done.2 = f32[256,256]{1,0:T(8,128)S(1)} copy-done((f32[256,256]{1,0:T(8,128)S(1)}, f32[256,256]{1,0:T(8,128)}, u32[]{:S(2)}) %copy-start.2) | copy-done | bytes 262168
  3.8 58.7 %band_update.1 = (f32[4096,128]{1,0:T(8,128)S(1)}, bf16[4,256,256]{2,1,0:T(8,128)(2,1)S(1)}, bf16[4,256,256]{2,1,0:T(8,128)(2,1)S(1)}, bf16[256,512]{1,0:T(8,128)(2,1)S(1)}, bf16[256,512]{1,0:T(8,128)(2,1)S(1)}) custom-call(f32[4096,128]{1,0:T(8,128)S(1)} %bitcast.3, f32[4,256,256]{2,1,0:T(8,128)S(1)} %bitcast.4, f32[256,256]{1,0:T(8,128)S(1)} %copy-done.2), custom_call_target="tpu_custom_call" | custom-call | tf_op jit(solution)/shard_map/band_update/pallas_call | solution.py:282
  62.5 4.2 %band_finish.1 = f32[4096,128]{1,0:T(8,128)} custom-call(f32[4096,128]{1,0:T(8,128)S(1)} %get-tuple-element.10.o_ref, bf16[4,256,256]{2,1,0:T(8,128)(2,1)S(1)} %get-tuple-element.11.uh_ref, bf16[4,256,256]{2,1,0:T(8,128)(2,1)S(1)} %get-tuple-element.12.ul_ref, bf16[256,512]{1,0:T(8,128)(2,1)S(1)} %get-tuple-element.13.wh_ref, ...), custom_call_target="tpu_custom_call" | custom-call | tf_op jit(solution)/shard_map/band_finish/pallas_call | solution.py:308
Async XLA Ops:
  0.0 1.6 %copy-start = (f32[4,1,256,2,1,256]{5,4,3,2,1,0:T(1,128)S(1)}, f32[4,1,256,2,1,256]{5,4,3,2,1,0:T(1,128)}, u32[]{:S(2)}) copy-start(f32[4,1,256,2,1,256]{5,4,3,2,1,0:T(1,128)} %param.3) | copy-start | bytes 6291460
  1.6 1.2 %copy-start.1 = (f32[4,1,256,256]{3,2,1,0:T(8,128)S(1)}, f32[4,1,256,256]{3,2,1,0:T(8,128)}, u32[]{:S(2)}) copy-start(f32[4,1,256,256]{3,2,1,0:T(8,128)} %param.4) | copy-start | bytes 3145732
  2.8 0.9 %copy-start.2 = (f32[256,256]{1,0:T(8,128)S(1)}, f32[256,256]{1,0:T(8,128)}, u32[]{:S(2)}) copy-start(f32[256,256]{1,0:T(8,128)} %t_s.1) | copy-start | bytes 786436

commit v3 on v2

--- a/solution.py
+++ b/solution.py
@@ -14,6 +14,14 @@
 VMEM_LIMIT = 24 * 1024 * 1024
 
 
+def rem(value, by):
+    return lax.rem(value, jnp.int32(by))
+
+
+def div(value, by):
+    return lax.div(value, jnp.int32(by))
+
+
 def split(value):
     high = value.astype(BF16)
     return high, (value - high.astype(F32)).astype(BF16)
@@ -33,39 +41,42 @@
 
 
 def kernel(
-    a_s, v_s, t_s, o_s, uh, ul, wh, wl,
+    a_hbm, v_hbm, t_hbm, o_s, uh, ul, wh, wl, a_s, v_s, t_s,
     vth, vtl, qt, xbuf, rsrc, rs, pct, prt, vc, uch, ucl, gsrc, gz, gsum, gx, gt,
-    one_s, one_r, v_s_s, v_s_r, rs_s, rs_r, y_s, y_r,
+    ld_sem, one_s, one_r, v_s_s, v_s_r, rs_s, rs_r, y_s, y_r,
     z_s, z_r, gz_s, gz_r, x_s, x_r, f_s, f_r, gx_s, gx_r,
 ):
     row = lax.axis_index("row")
     col = lax.axis_index("col")
-    y, j = row // 2, row % 2
-    z, x = col // X, col % X
-    half, pos = col // 16, col % 16
+    y, j = div(row, 2), rem(row, 2)
+    z, x = div(col, X), rem(col, X)
+    half, pos = div(col, 16), rem(col, 16)
+    zs = [rem(z + Z - d, Z) for d in range(Z)]
+    xs = [rem(x + d, X) for d in range(X)]
+    ys = [rem(y + d, Y) for d in range(Y)]
 
     def flip(index):
-        return index + 1 - 2 * (index % 2)
+        return index + 1 - 2 * rem(index, 2)
 
     def slice_at(position):
         other = flip(position)
-        return 8 * (other % 2) + other // 2
+        return 8 * rem(other, 2) + div(other, 2)
 
     mine, held = 8 * j + y, slice_at(pos)
     t_target, t_source = (pos, 16 * half + flip(row)), (flip(pos), 16 * half + row)
     partner = (2 * y + 1 - j, col)
 
     def y_peer(d):
-        return (2 * ((y + d) % Y) + j, col)
+        return (2 * ys[d] + j, col)
 
     def z_peer(d):
-        return (row, X * ((z + d) % Z) + x)
+        return (row, X * zs[Z - d] + x)
 
     def x_peer(d):
-        return (row, X * z + (x + d) % X)
+        return (row, X * z + xs[d % X])
 
     def v_target(d):
-        return (2 * ((held + d) % Y) + held // 8, 16 * half + row)
+        return (2 * rem(held + d, Y) + div(held, 8), 16 * half + row)
 
     def rows(start, size, step=16):
         return pl.ds(pl.multiple_of(start, step), size)
@@ -81,6 +92,12 @@
         started.append(copy)
         return copy
 
+    loads = [
+        pltpu.make_async_copy(src, dst, ld_sem.at[i])
+        for i, (src, dst) in enumerate([(v_hbm, v_s), (a_hbm, a_s), (t_hbm, t_s)])
+    ]
+    for copy in loads:
+        copy.start()
     barrier = pltpu.get_barrier_semaphore()
     greeted = (
         [y_peer(d) for d in range(1, Y)] + [z_peer(d) for d in range(1, Z)]
@@ -92,6 +109,7 @@
             barrier, inc=1, device_id={"row": peer[0], "col": peer[1]}, device_id_type=MESH
         )
 
+    loads[0].wait()
     for lr in range(4):
         block = v_s[lr]
         if lr == 0:
@@ -103,6 +121,8 @@
         uh[lr] = high
         ul[lr] = low
 
+    loads[1].wait()
+
     def partial(lc):
         block = jnp.concatenate(
             [a_s[pl.ds(2 * lc + q, 1024, stride=4), :] for q in range(2)], axis=1
@@ -120,7 +140,7 @@
     partial(0)
     pl.semaphore_wait(barrier, len(greeted))
     swaps = [swap_of(0)]
-    v_part = v_s.at[half + 2 * (held // 8), rows(32 * (held % 8), 32)]
+    v_part = v_s.at[half + 2 * div(held, 8), rows(32 * rem(held, 8), 32)]
     v_moves = [
         send(v_part, vc.at[rows(32 * held, 32)], v_s_s.at[d], v_s_r.at[d], v_target(d))
         for d in range(8)
@@ -133,17 +153,19 @@
         rsrc[lc] = qt[lc, rows(128 * j, 128), :] + xbuf[lc]
         scatter.append([
             send(
-                rsrc.at[lc, rows(16 * ((y + d) % Y), 16)], rs.at[lc, d],
+                rsrc.at[lc, rows(16 * ys[d], 16)], rs.at[lc, d],
                 rs_s.at[lc, d], rs_r.at[lc, d], y_peer(d),
             )
             for d in order
         ])
+    loads[2].wait()
     factor = split(t_s[...])
     for lr in range(4):
         high, low = split(dot3((uh[lr], ul[lr]), factor, NT))
         uh[lr] = high
         ul[lr] = low
     own = rows(16 * mine, 16)
+    t_z, t_x = 4 * half + div(flip(row), X), rem(flip(row), X)
     totals, t_moves = [], []
     for lc in range(2):
         total = rsrc[lc, rows(16 * y, 16), :]
@@ -153,7 +175,7 @@
         pct[lc, own, :] = total
         totals.append(total)
         t_moves.append(send(
-            pct.at[lc, own], prt.at[half, lc, own], one_s.at[2 + lc], one_r.at[2 + lc], t_target
+            pct.at[lc, own], prt.at[lc, t_z, t_x], one_s.at[2 + lc], one_r.at[2 + lc], t_target
         ))
     p_part = pct.at[:, own]
     p_gather = [
@@ -174,11 +196,8 @@
         uch[:, 256 * lc : 256 * lc + 256] = high
         ucl[:, 256 * lc : 256 * lc + 256] = low
 
-    def chunk_of(zi, xi, lc):
-        return prt.at[zi // 4, lc, rows(16 * slice_at(4 * (zi % 4) + xi), 16)]
-
     def x_send(d, lc):
-        part = chunk_of((z - d) % Z, x, lc)
+        part = prt.at[lc, zs[d], x]
         return [
             send(part, part, x_s.at[side, lc, d], x_r.at[side, lc, d], x_peer(1 - 2 * side))
             for side in range(2)
@@ -187,7 +206,7 @@
     z_gather, x_gather = [], [{}, {}]
     for lc in range(2):
         t_moves[lc].wait_recv()
-        chunk = chunk_of(z, x, lc)
+        chunk = prt.at[lc, z, x]
         z_gather.append({
             d: send(chunk, chunk, z_s.at[lc, d], z_r.at[lc, d], z_peer(d)) for d in order
         })
@@ -197,7 +216,7 @@
 
     def pass_on(d, lc):
         x_gather[lc][d][lc].wait_recv()
-        part = chunk_of((z - d) % Z, (x - 1 + 2 * lc) % X, lc)
+        part = prt.at[lc, zs[d], xs[3 - 2 * lc]]
         forward[lc].append(
             send(part, part, f_s.at[lc, d], f_r.at[lc, d], x_peer(1 - 2 * lc))
         )
@@ -232,6 +251,7 @@
     p_half = pct.at[:, rows(128 * j, 128)]
     p_swap = send(p_half, p_half, one_s.at[5], one_r.at[5], partner)
 
+    places = [(2 * (e % 8) + e // 8) ^ 1 for e in range(16)]
     for lc in range(2):
         for d in (0,) + near:
             x_gather[lc][d][1 - lc].wait_recv()
@@ -239,7 +259,9 @@
             copy.wait_recv()
         for h in range(2):
             lr = h + 2 * lc
-            left = split(prt[h, lc].T)
+            left = split(jnp.concatenate(
+                [prt[lc, 4 * h + p // X, p % X] for p in places], axis=0
+            ).T)
             for oc in range(2):
                 cols = slice(256 * oc, 256 * oc + 256)
                 delta = dot3(left, (uch[:, cols], ucl[:, cols]), NN)
@@ -262,15 +284,25 @@
         copy.wait_send()
 
 
-def finish_kernel(o_ref, uh_ref, ul_ref, wh_ref, wl_ref, out_ref):
-    left = (uh_ref[0], ul_ref[0])
-    count = left[0].shape[0]
-    for oc in range(2):
-        cols = slice(256 * oc, 256 * oc + 256)
-        delta = dot3(left, (wh_ref[:, cols], wl_ref[:, cols]), NN)
-        for q in range(2):
-            where = pl.ds(2 * oc + q, count, stride=4)
-            out_ref[where, :] = o_ref[where, :] - delta[:, 128 * q : 128 * q + 128]
+def finish_kernel(o_ref, uh_ref, ul_ref, wh_ref, wl_ref, out_hbm, buf, sems):
+    def store(lr):
+        part = pl.ds(1024 * lr, 1024)
+        return pltpu.make_async_copy(buf.at[part], out_hbm.at[part], sems.at[lr])
+
+    right = [
+        (wh_ref[:, 256 * oc : 256 * oc + 256], wl_ref[:, 256 * oc : 256 * oc + 256])
+        for oc in range(2)
+    ]
+    for lr in range(4):
+        left = (uh_ref[lr], ul_ref[lr])
+        for oc in range(2):
+            delta = dot3(left, right[oc], NN)
+            for q in range(2):
+                where = pl.ds(1024 * lr + 2 * oc + q, 256, stride=4)
+                buf[where, :] = o_ref[where, :] - delta[:, 128 * q : 128 * q + 128]
+        store(lr).start()
+    for lr in range(4):
+        store(lr).wait()
 
 
 def per_device(matrix, vectors, t_factor):
@@ -285,16 +317,17 @@
             shape((4096, 128), F32), shape((4, 256, 256), BF16), shape((4, 256, 256), BF16),
             shape((256, 512), BF16), shape((256, 512), BF16),
         ],
-        in_specs=[pl.BlockSpec(memory_space=pltpu.VMEM)] * 3,
+        in_specs=[pl.BlockSpec(memory_space=pl.ANY)] * 3,
         out_specs=[pl.BlockSpec(memory_space=pltpu.VMEM)] * 5,
         scratch_shapes=[
+            vm((4096, 128), F32), vm((4, 256, 256), F32), vm((256, 256), F32),
             vm((256, 1024), BF16), vm((256, 1024), BF16),
             vm((2, 256, 256), F32), vm((2, 128, 256), F32), vm((2, 128, 256), F32),
-            vm((2, 8, 16, 256), F32), vm((2, 256, 256), F32), vm((2, 2, 256, 256), F32),
+            vm((2, 8, 16, 256), F32), vm((2, 256, 256), F32), vm((2, 8, 4, 16, 256), F32),
             vm((512, 256), F32), vm((256, 512), BF16), vm((256, 512), BF16),
             vm((16, 256), F32), vm((8, 16, 256), F32), vm((16, 256), F32),
             vm((4, 16, 256), F32), vm((256, 256), F32),
-            dma((7,)), dma((7,)), dma((8,)), dma((8,)),
+            dma((3,)), dma((7,)), dma((7,)), dma((8,)), dma((8,)),
             dma((2, 8)), dma((2, 8)), dma((2, 8)), dma((2, 8)),
             dma((2, 8)), dma((2, 8)), dma((8,)), dma((8,)),
             dma((2, 2, 8)), dma((2, 2, 8)), dma((2, 8)), dma((2, 8)), dma((4,)), dma((4,)),
@@ -303,20 +336,13 @@
             collective_id=0, has_side_effects=True, vmem_limit_bytes=VMEM_LIMIT
         ),
         name="band_update",
-    )(a, v, t_factor)
-    steps = 8
+    )(*[pltpu.with_memory_space_constraint(arg, pltpu.HBM) for arg in (a, v, t_factor)])
     out = pl.pallas_call(
         finish_kernel,
-        grid=(steps,),
         out_shape=shape((4096, 128), F32),
-        in_specs=[
-            pl.BlockSpec((4096 // steps, 128), lambda i: (i, 0)),
-            pl.BlockSpec((1, 1024 // steps, 256), lambda i: (i // 2, i % 2, 0)),
-            pl.BlockSpec((1, 1024 // steps, 256), lambda i: (i // 2, i % 2, 0)),
-            pl.BlockSpec((256, 512), lambda i: (0, 0)),
-            pl.BlockSpec((256, 512), lambda i: (0, 0)),
-        ],
-        out_specs=pl.BlockSpec((4096 // steps, 128), lambda i: (i, 0)),
+        in_specs=[pl.BlockSpec(memory_space=pltpu.VMEM)] * 5,
+        out_specs=pl.BlockSpec(memory_space=pl.ANY),
+        scratch_shapes=[vm((4096, 128), F32), dma((4,))],
         compiler_params=pltpu.CompilerParams(vmem_limit_bytes=VMEM_LIMIT // 2),
         name="band_finish",
     )(*parts)

time: 66.9 us -> 60.1 us (0.90)
  local copies, waits for them, and re-layouts: 3.76 us -> 0 us
  Pallas kernels: 62.9 us -> 60 us
    unnamed x6 -> x0, local copies, waits for them, and re-layouts: 3.76 us -> none
    pallas_call x1, Pallas kernels: 4.21 us -> 1.83 us  [per_device(): pl.pallas_call(finish_kernel, out_shape=shape((4096, 128), F32), in_specs...]
where the time goes in v3:
time: 60.1 us; the launch traced here: 60 us
  Pallas kernels  60 us (100%)
    pallas_call x1, Pallas kernels, per_device(): pl.pallas_call(kernel, out_shape=[shape((4096, 128), F32), shape((4, 256,...  58.2 us
    pallas_call x1, Pallas kernels, per_device(): pl.pallas_call(finish_kernel, out_shape=shape((4096, 128), F32), in_specs...  1.83 us

profile of v3, /device:TPU:1, one launch (start us, length us, event | category | flops | bytes accessed | tf_op | source)
XLA Modules:
  0.0 60.0 jit_solution(15940080453590870897)
XLA Ops:
  0.0 58.2 %band_update.1 = (f32[4096,128]{1,0:T(8,128)S(1)}, bf16[4,256,256]{2,1,0:T(8,128)(2,1)S(1)}, bf16[4,256,256]{2,1,0:T(8,128)(2,1)S(1)}, bf16[256,512]{1,0:T(8,128)(2,1)S(1)}, bf16[256,512]{1,0:T(8,128)(2,1)S(1)}) custom-call(f32[4096,128]{1,0:T(8,128)} %bitcast.3, f32[4,256,256]{2,1,0:T(8,128)} %bitcast.4, f32[256,256]{1,0:T(8,128)} %t_hbm.1), custom_call_target="tpu_custom_call" | custom-call | tf_op jit(solution)/shard_map/band_update/pallas_call | solution.py:314
  58.2 1.8 %band_finish.1 = f32[4096,128]{1,0:T(8,128)} custom-call(f32[4096,128]{1,0:T(8,128)S(1)} %get-tuple-element.10.o_ref, bf16[4,256,256]{2,1,0:T(8,128)(2,1)S(1)} %get-tuple-element.11.uh_ref, bf16[4,256,256]{2,1,0:T(8,128)(2,1)S(1)} %get-tuple-element.12.ul_ref, bf16[256,512]{1,0:T(8,128)(2,1)S(1)} %get-tuple-element.13.wh_ref, ...), custom_call_target="tpu_custom_call" | custom-call | tf_op jit(solution)/shard_map/band_finish/pallas_call | solution.py:340

commit v4 on v3

--- a/solution.py
+++ b/solution.py
@@ -177,14 +177,30 @@
         t_moves.append(send(
             pct.at[lc, own], prt.at[lc, t_z, t_x], one_s.at[2 + lc], one_r.at[2 + lc], t_target
         ))
+    for copy in v_moves:
+        copy.wait_recv()
+    v_half = vc.at[rows(256 * j, 256)]
+    v_swap = send(v_half, v_half, one_s.at[4], one_r.at[4], partner)
+    def x_send(d, lc):
+        part = prt.at[lc, zs[d], x]
+        return [
+            send(part, part, x_s.at[side, lc, d], x_r.at[side, lc, d], x_peer(1 - 2 * side))
+            for side in range(2)
+        ]
+
+    near = (1, 7, 2, 6, 3, 5, 4)
+    z_gather, x_gather = [], [{}, {}]
+    for lc in range(2):
+        t_moves[lc].wait_recv()
+        chunk = prt.at[lc, z, x]
+        z_gather.append({
+            d: send(chunk, chunk, z_s.at[lc, d], z_r.at[lc, d], z_peer(d)) for d in near
+        })
+        x_gather[lc][0] = x_send(0, lc)
     p_part = pct.at[:, own]
     p_gather = [
         send(p_part, p_part, y_s.at[0, d], y_r.at[0, d], y_peer(d)) for d in order
     ]
-    for copy in v_moves:
-        copy.wait_recv()
-    v_half = vc.at[rows(256 * j, 256)]
-    v_swap = send(v_half, v_half, one_s.at[4], one_r.at[4], partner)
     v_swap.wait_recv()
     first = vc[0:256, :]
     first = jnp.where(col == 0, unit_lower(first), first)
@@ -196,22 +212,6 @@
         uch[:, 256 * lc : 256 * lc + 256] = high
         ucl[:, 256 * lc : 256 * lc + 256] = low
 
-    def x_send(d, lc):
-        part = prt.at[lc, zs[d], x]
-        return [
-            send(part, part, x_s.at[side, lc, d], x_r.at[side, lc, d], x_peer(1 - 2 * side))
-            for side in range(2)
-        ]
-
-    z_gather, x_gather = [], [{}, {}]
-    for lc in range(2):
-        t_moves[lc].wait_recv()
-        chunk = prt.at[lc, z, x]
-        z_gather.append({
-            d: send(chunk, chunk, z_s.at[lc, d], z_r.at[lc, d], z_peer(d)) for d in order
-        })
-        x_gather[lc][0] = x_send(0, lc)
-    near = (1, 7, 2, 6, 3, 5, 4)
     forward = [[], []]
 
     def pass_on(d, lc):
@@ -224,9 +224,10 @@
     for d in near:
         z_gather[0][d].wait_recv()
         x_gather[0][d] = x_send(d, 0)
-    for d in near:
+    for d, e in zip(near, (0,) + near):
         z_gather[1][d].wait_recv()
         x_gather[1][d] = x_send(d, 1)
+        pass_on(e, 0)
     part_sum = gsrc[...]
     for copy, d in zip(g_z, order):
         copy.wait_recv()
@@ -235,8 +236,7 @@
     g_x = [
         send(gsum, gx.at[d], gx_s.at[d], gx_r.at[d], x_peer(d)) for d in range(1, X)
     ]
-    for d in (0,) + near:
-        pass_on(d, 0)
+    pass_on(near[-1], 0)
     for d in (0,) + near:
         pass_on(d, 1)
     for d, copy in zip(range(1, X), g_x):

time: 60.1 us -> 61.1 us (1.017)
  Pallas kernels: 60 us -> 61 us
    pallas_call x1, Pallas kernels: 58.2 us -> 59.2 us  [per_device(): pl.pallas_call(kernel, out_shape=[shape((4096, 128), F32), shape((4, 256,...]
where the time goes in v4:
time: 61.1 us; the launch traced here: 61 us
  Pallas kernels  61 us (100%)
    pallas_call x1, Pallas kernels, per_device(): pl.pallas_call(kernel, out_shape=[shape((4096, 128), F32), shape((4, 256,...  59.2 us
    pallas_call x1, Pallas kernels, per_device(): pl.pallas_call(finish_kernel, out_shape=shape((4096, 128), F32), in_specs...  1.83 us

profile of v4, /device:TPU:1, one launch (start us, length us, event | category | flops | bytes accessed | tf_op | source)
XLA Modules:
  0.0 61.0 jit_solution(2439083356437082878)
XLA Ops:
  0.0 59.2 %band_update.1 = (f32[4096,128]{1,0:T(8,128)S(1)}, bf16[4,256,256]{2,1,0:T(8,128)(2,1)S(1)}, bf16[4,256,256]{2,1,0:T(8,128)(2,1)S(1)}, bf16[256,512]{1,0:T(8,128)(2,1)S(1)}, bf16[256,512]{1,0:T(8,128)(2,1)S(1)}) custom-call(f32[4096,128]{1,0:T(8,128)} %bitcast.3, f32[4,256,256]{2,1,0:T(8,128)} %bitcast.4, f32[256,256]{1,0:T(8,128)} %t_hbm.1), custom_call_target="tpu_custom_call" | custom-call | tf_op jit(solution)/shard_map/band_update/pallas_call | solution.py:314
  59.2 1.8 %band_finish.1 = f32[4096,128]{1,0:T(8,128)} custom-call(f32[4096,128]{1,0:T(8,128)S(1)} %get-tuple-element.10.o_ref, bf16[4,256,256]{2,1,0:T(8,128)(2,1)S(1)} %get-tuple-element.11.uh_ref, bf16[4,256,256]{2,1,0:T(8,128)(2,1)S(1)} %get-tuple-element.12.ul_ref, bf16[256,512]{1,0:T(8,128)(2,1)S(1)} %get-tuple-element.13.wh_ref, ...), custom_call_target="tpu_custom_call" | custom-call | tf_op jit(solution)/shard_map/band_finish/pallas_call | solution.py:340

commit v5 on v3

--- a/solution.py
+++ b/solution.py
@@ -164,6 +164,10 @@
         high, low = split(dot3((uh[lr], ul[lr]), factor, NT))
         uh[lr] = high
         ul[lr] = low
+    for copy in v_moves:
+        copy.wait_recv()
+    v_half = vc.at[rows(256 * j, 256)]
+    v_swap = send(v_half, v_half, one_s.at[4], one_r.at[4], partner)
     own = rows(16 * mine, 16)
     t_z, t_x = 4 * half + div(flip(row), X), rem(flip(row), X)
     totals, t_moves = [], []
@@ -177,20 +181,16 @@
         t_moves.append(send(
             pct.at[lc, own], prt.at[lc, t_z, t_x], one_s.at[2 + lc], one_r.at[2 + lc], t_target
         ))
-    p_part = pct.at[:, own]
-    p_gather = [
-        send(p_part, p_part, y_s.at[0, d], y_r.at[0, d], y_peer(d)) for d in order
-    ]
-    for copy in v_moves:
-        copy.wait_recv()
-    v_half = vc.at[rows(256 * j, 256)]
-    v_swap = send(v_half, v_half, one_s.at[4], one_r.at[4], partner)
     v_swap.wait_recv()
     first = vc[0:256, :]
     first = jnp.where(col == 0, unit_lower(first), first)
     v_cols = [split(first), split(vc[256:512, :])]
     gsrc[...] = dot3(split(totals[0]), v_cols[0], NN) + dot3(split(totals[1]), v_cols[1], NN)
     g_z = [send(gsrc, gz.at[d], gz_s.at[d], gz_r.at[d], z_peer(d)) for d in order]
+    p_part = pct.at[:, own]
+    p_gather = [
+        send(p_part, p_part, y_s.at[0, d], y_r.at[0, d], y_peer(d)) for d in order
+    ]
     for lc in range(2):
         high, low = split(dot3(factor, v_cols[lc], NT))
         uch[:, 256 * lc : 256 * lc + 256] = high
@@ -203,15 +203,24 @@
             for side in range(2)
         ]
 
+    near = (1, 7, 2, 6, 3, 5, 4)
     z_gather, x_gather = [], [{}, {}]
     for lc in range(2):
         t_moves[lc].wait_recv()
         chunk = prt.at[lc, z, x]
         z_gather.append({
-            d: send(chunk, chunk, z_s.at[lc, d], z_r.at[lc, d], z_peer(d)) for d in order
+            d: send(chunk, chunk, z_s.at[lc, d], z_r.at[lc, d], z_peer(d)) for d in near
         })
         x_gather[lc][0] = x_send(0, lc)
-    near = (1, 7, 2, 6, 3, 5, 4)
+    part_sum = gsrc[...]
+    for copy, d in zip(g_z, order):
+        copy.wait_recv()
+        part_sum = part_sum + gz[d]
+    gsum[...] = part_sum
+    g_x = [
+        send(gsum, gx.at[d], gx_s.at[d], gx_r.at[d], x_peer(d)) for d in range(1, X)
+    ]
+
     forward = [[], []]
 
     def pass_on(d, lc):
@@ -224,21 +233,6 @@
     for d in near:
         z_gather[0][d].wait_recv()
         x_gather[0][d] = x_send(d, 0)
-    for d in near:
-        z_gather[1][d].wait_recv()
-        x_gather[1][d] = x_send(d, 1)
-    part_sum = gsrc[...]
-    for copy, d in zip(g_z, order):
-        copy.wait_recv()
-        part_sum = part_sum + gz[d]
-    gsum[...] = part_sum
-    g_x = [
-        send(gsum, gx.at[d], gx_s.at[d], gx_r.at[d], x_peer(d)) for d in range(1, X)
-    ]
-    for d in (0,) + near:
-        pass_on(d, 0)
-    for d in (0,) + near:
-        pass_on(d, 1)
     for d, copy in zip(range(1, X), g_x):
         copy.wait_recv()
         part_sum = part_sum + gx[d]
@@ -246,11 +240,22 @@
     g_gather = [
         send(gt.at[own], gt.at[own], y_s.at[1, d], y_r.at[1, d], y_peer(d)) for d in order
     ]
+    for d, e in zip(near, (0,) + near):
+        z_gather[1][d].wait_recv()
+        x_gather[1][d] = x_send(d, 1)
+        pass_on(e, 0)
+    pass_on(near[-1], 0)
+    for d in (0,) + near:
+        pass_on(d, 1)
     for copy in p_gather:
         copy.wait_recv()
     p_half = pct.at[:, rows(128 * j, 128)]
     p_swap = send(p_half, p_half, one_s.at[5], one_r.at[5], partner)
 
+    for copy in g_gather:
+        copy.wait_recv()
+    g_half = gt.at[rows(128 * j, 128)]
+    g_swap = send(g_half, g_half, one_s.at[6], one_r.at[6], partner)
     places = [(2 * (e % 8) + e // 8) ^ 1 for e in range(16)]
     for lc in range(2):
         for d in (0,) + near:
@@ -268,10 +273,6 @@
                 for q in range(2):
                     where = pl.ds(lr * 1024 + 2 * oc + q, 256, stride=4)
                     o_s[where, :] = a_s[where, :] - delta[:, 128 * q : 128 * q + 128]
-    for copy in g_gather:
-        copy.wait_recv()
-    g_half = gt.at[rows(128 * j, 128)]
-    g_swap = send(g_half, g_half, one_s.at[6], one_r.at[6], partner)
     p_swap.wait_recv()
     g_swap.wait_recv()
     inner = split(gt[...])

time: 60.1 us -> 56.5 us (0.940)
  the two profiles are of different devices: /device:TPU:1 before, /device:TPU:8 now
where the time goes in v5:
time: 56.5 us; the launch traced here: 56.3 us
  Pallas kernels  56.3 us (100%)
    pallas_call x1, Pallas kernels, per_device(): pl.pallas_call(kernel, out_shape=[shape((4096, 128), F32), shape((4, 256,...  54.5 us
    pallas_call x1, Pallas kernels, per_device(): pl.pallas_call(finish_kernel, out_shape=shape((4096, 128), F32), in_specs...  1.83 us

profile of v5, /device:TPU:8, one launch (start us, length us, event | category | flops | bytes accessed | tf_op | source)
XLA Modules:
  0.0 56.3 jit_solution(15508200923151410275)
XLA Ops:
  0.0 54.5 %band_update.1 = (f32[4096,128]{1,0:T(8,128)S(1)}, bf16[4,256,256]{2,1,0:T(8,128)(2,1)S(1)}, bf16[4,256,256]{2,1,0:T(8,128)(2,1)S(1)}, bf16[256,512]{1,0:T(8,128)(2,1)S(1)}, bf16[256,512]{1,0:T(8,128)(2,1)S(1)}) custom-call(f32[4096,128]{1,0:T(8,128)} %bitcast.3, f32[4,256,256]{2,1,0:T(8,128)} %bitcast.4, f32[256,256]{1,0:T(8,128)} %t_hbm.1), custom_call_target="tpu_custom_call" | custom-call | tf_op jit(solution)/shard_map/band_update/pallas_call | solution.py:315
  54.5 1.8 %band_finish.1 = f32[4096,128]{1,0:T(8,128)} custom-call(f32[4096,128]{1,0:T(8,128)S(1)} %get-tuple-element.10.o_ref, bf16[4,256,256]{2,1,0:T(8,128)(2,1)S(1)} %get-tuple-element.11.uh_ref, bf16[4,256,256]{2,1,0:T(8,128)(2,1)S(1)} %get-tuple-element.12.ul_ref, bf16[256,512]{1,0:T(8,128)(2,1)S(1)} %get-tuple-element.13.wh_ref, ...), custom_call_target="tpu_custom_call" | custom-call | tf_op jit(solution)/shard_map/band_finish/pallas_call | solution.py:341

commit v6 on v5

--- a/solution.py
+++ b/solution.py
@@ -42,7 +42,7 @@
 
 def kernel(
     a_hbm, v_hbm, t_hbm, o_s, uh, ul, wh, wl, a_s, v_s, t_s,
-    vth, vtl, qt, xbuf, rsrc, rs, pct, prt, vc, uch, ucl, gsrc, gz, gsum, gx, gt,
+    vth, vtl, qt, xbuf, rsrc, rs, cmb, pct, prt, vc, uch, ucl, gsrc, gz, gsum, gx, gt,
     ld_sem, one_s, one_r, v_s_s, v_s_r, rs_s, rs_r, y_s, y_r,
     z_s, z_r, gz_s, gz_r, x_s, x_r, f_s, f_r, gx_s, gx_r,
 ):
@@ -147,40 +147,54 @@
     ]
     partial(1)
     swaps.append(swap_of(1))
-    scatter = []
+    def own_part(lc, d):
+        return rsrc[lc, rows(16 * ys[d % Y], 16), :]
+
+    def scatter(lc, slot, src, d):
+        hops[lc][slot] = send(
+            src, rs.at[lc, slot], rs_s.at[lc, slot], rs_r.at[lc, slot], y_peer(d)
+        )
+
+    def add_and_pass(lc, arrived, chunk, slot, d):
+        hops[lc][arrived].wait_recv()
+        part = cmb.at[lc, slot - 4]
+        part[...] = own_part(lc, chunk) + rs[lc, arrived]
+        scatter(lc, slot, part, d)
+
+    hops = [{}, {}]
     for lc in range(2):
         swaps[lc].wait_recv()
         rsrc[lc] = qt[lc, rows(128 * j, 128), :] + xbuf[lc]
-        scatter.append([
-            send(
-                rsrc.at[lc, rows(16 * ys[d], 16)], rs.at[lc, d],
-                rs_s.at[lc, d], rs_r.at[lc, d], y_peer(d),
-            )
-            for d in order
-        ])
+        for slot, chunk, d in ((0, -4, 7), (1, 3, 1), (2, -1, 7), (3, 1, 1)):
+            scatter(lc, slot, rsrc.at[lc, rows(16 * ys[chunk % Y], 16)], d)
     loads[2].wait()
     factor = split(t_s[...])
     for lr in range(4):
         high, low = split(dot3((uh[lr], ul[lr]), factor, NT))
         uh[lr] = high
         ul[lr] = low
-    for copy in v_moves:
-        copy.wait_recv()
-    v_half = vc.at[rows(256 * j, 256)]
-    v_swap = send(v_half, v_half, one_s.at[4], one_r.at[4], partner)
     own = rows(16 * mine, 16)
     t_z, t_x = 4 * half + div(flip(row), X), rem(flip(row), X)
+    for lc in range(2):
+        add_and_pass(lc, 0, -3, 4, 7)
+        add_and_pass(lc, 1, 2, 5, 2)
+    for lc in range(2):
+        add_and_pass(lc, 4, -2, 6, 6)
     totals, t_moves = [], []
     for lc in range(2):
-        total = rsrc[lc, rows(16 * y, 16), :]
-        for copy, d in zip(scatter[lc], order):
-            copy.wait_recv()
-            total = total + rs[lc, d]
+        total = own_part(lc, 0)
+        for slot in (2, 3, 5, 6):
+            hops[lc][slot].wait_recv()
+            total = total + rs[lc, slot]
         pct[lc, own, :] = total
         totals.append(total)
         t_moves.append(send(
             pct.at[lc, own], prt.at[lc, t_z, t_x], one_s.at[2 + lc], one_r.at[2 + lc], t_target
         ))
+    for copy in v_moves:
+        copy.wait_recv()
+    v_half = vc.at[rows(256 * j, 256)]
+    v_swap = send(v_half, v_half, one_s.at[4], one_r.at[4], partner)
     v_swap.wait_recv()
     first = vc[0:256, :]
     first = jnp.where(col == 0, unit_lower(first), first)
@@ -324,7 +338,7 @@
             vm((4096, 128), F32), vm((4, 256, 256), F32), vm((256, 256), F32),
             vm((256, 1024), BF16), vm((256, 1024), BF16),
             vm((2, 256, 256), F32), vm((2, 128, 256), F32), vm((2, 128, 256), F32),
-            vm((2, 8, 16, 256), F32), vm((2, 256, 256), F32), vm((2, 8, 4, 16, 256), F32),
+            vm((2, 8, 16, 256), F32), vm((2, 3, 16, 256), F32), vm((2, 256, 256), F32), vm((2, 8, 4, 16, 256), F32),
             vm((512, 256), F32), vm((256, 512), BF16), vm((256, 512), BF16),
             vm((16, 256), F32), vm((8, 16, 256), F32), vm((16, 256), F32),
             vm((4, 16, 256), F32), vm((256, 256), F32),

time: 56.5 us -> 56.9 us (level)
  the two profiles are of different devices: /device:TPU:8 before, /device:TPU:1 now
where the time goes in v6:
time: 56.9 us; the launch traced here: 56.4 us
  Pallas kernels  56.4 us (99%)
    pallas_call x1, Pallas kernels, per_device(): pl.pallas_call(kernel, out_shape=[shape((4096, 128), F32), shape((4, 256,...  54.6 us
    pallas_call x1, Pallas kernels, per_device(): pl.pallas_call(finish_kernel, out_shape=shape((4096, 128), F32), in_specs...  1.83 us

profile of v6, /device:TPU:1, one launch (start us, length us, event | category | flops | bytes accessed | tf_op | source)
XLA Modules:
  0.0 56.4 jit_solution(9842745181888016498)
XLA Ops:
  0.0 54.6 %band_update.1 = (f32[4096,128]{1,0:T(8,128)S(1)}, bf16[4,256,256]{2,1,0:T(8,128)(2,1)S(1)}, bf16[4,256,256]{2,1,0:T(8,128)(2,1)S(1)}, bf16[256,512]{1,0:T(8,128)(2,1)S(1)}, bf16[256,512]{1,0:T(8,128)(2,1)S(1)}) custom-call(f32[4096,128]{1,0:T(8,128)} %bitcast.3, f32[4,256,256]{2,1,0:T(8,128)} %bitcast.4, f32[256,256]{1,0:T(8,128)} %t_hbm.1), custom_call_target="tpu_custom_call" | custom-call | tf_op jit(solution)/shard_map/band_update/pallas_call | solution.py:329
  54.6 1.8 %band_finish.1 = f32[4096,128]{1,0:T(8,128)} custom-call(f32[4096,128]{1,0:T(8,128)S(1)} %get-tuple-element.10.o_ref, bf16[4,256,256]{2,1,0:T(8,128)(2,1)S(1)} %get-tuple-element.11.uh_ref, bf16[4,256,256]{2,1,0:T(8,128)(2,1)S(1)} %get-tuple-element.12.ul_ref, bf16[256,512]{1,0:T(8,128)(2,1)S(1)} %get-tuple-element.13.wh_ref, ...), custom_call_target="tpu_custom_call" | custom-call | tf_op jit(solution)/shard_map/band_finish/pallas_call | solution.py:355

commit v7 on v6

--- a/solution.py
+++ b/solution.py
@@ -43,7 +43,7 @@
 def kernel(
     a_hbm, v_hbm, t_hbm, o_s, uh, ul, wh, wl, a_s, v_s, t_s,
     vth, vtl, qt, xbuf, rsrc, rs, cmb, pct, prt, vc, uch, ucl, gsrc, gz, gsum, gx, gt,
-    ld_sem, one_s, one_r, v_s_s, v_s_r, rs_s, rs_r, y_s, y_r,
+    ld_sem, one_s, one_r, v_s_s, v_s_r, v_l, vg_s, vg_r, rs_s, rs_r, y_s, y_r,
     z_s, z_r, gz_s, gz_r, x_s, x_r, f_s, f_r, gx_s, gx_r,
 ):
     row = lax.axis_index("row")
@@ -58,11 +58,7 @@
     def flip(index):
         return index + 1 - 2 * rem(index, 2)
 
-    def slice_at(position):
-        other = flip(position)
-        return 8 * rem(other, 2) + div(other, 2)
-
-    mine, held = 8 * j + y, slice_at(pos)
+    mine = 8 * j + y
     t_target, t_source = (pos, 16 * half + flip(row)), (flip(pos), 16 * half + row)
     partner = (2 * y + 1 - j, col)
 
@@ -75,8 +71,22 @@
     def x_peer(d):
         return (row, X * z + xs[d % X])
 
-    def v_target(d):
-        return (2 * rem(held + d, Y) + div(held, 8), 16 * half + row)
+    owner = row == pos
+
+    def v_piece(d, lane):
+        return v_s.at[half + 2 * lane, rows(32 * ys[d], 32)], 256 * lane + 32 * ys[d]
+
+    def v_scatter(d, lane, same):
+        src, start = v_piece(d, lane)
+        return pltpu.make_async_remote_copy(
+            src_ref=src, dst_ref=vc.at[rows(start, 32)],
+            send_sem=v_s_s.at[d, same], recv_sem=v_s_r,
+            device_id={"row": 2 * ys[d] + lane, "col": col}, device_id_type=MESH,
+        )
+
+    def v_local():
+        src, start = v_piece(0, j)
+        return pltpu.make_async_copy(src, vc.at[rows(start, 32)], v_l)
 
     def rows(start, size, step=16):
         return pl.ds(pl.multiple_of(start, step), size)
@@ -102,7 +112,7 @@
     greeted = (
         [y_peer(d) for d in range(1, Y)] + [z_peer(d) for d in range(1, Z)]
         + [x_peer(d) for d in range(1, X)] + [partner, t_source]
-        + [(pos, 16 * half + 2 * i + 1 - j) for i in range(8)]
+        + [(2 * ys[d] + 1 - j, col) for d in range(1, Y)]
     )
     for peer in greeted:
         pl.semaphore_signal(
@@ -140,11 +150,15 @@
     partial(0)
     pl.semaphore_wait(barrier, len(greeted))
     swaps = [swap_of(0)]
-    v_part = v_s.at[half + 2 * div(held, 8), rows(32 * rem(held, 8), 32)]
-    v_moves = [
-        send(v_part, vc.at[rows(32 * held, 32)], v_s_s.at[d], v_s_r.at[d], v_target(d))
-        for d in range(8)
-    ]
+
+    @pl.when(owner)
+    def _():
+        v_local().start()
+        for d in (4, 3, 5, 2, 6, 1, 7, 0):
+            v_scatter(d, 1 - j, 1).start()
+            if d:
+                v_scatter(d, j, 0).start()
+
     partial(1)
     swaps.append(swap_of(1))
     def own_part(lc, d):
@@ -180,6 +194,23 @@
         add_and_pass(lc, 1, 2, 5, 2)
     for lc in range(2):
         add_and_pass(lc, 4, -2, 6, 6)
+    @pl.when(owner)
+    def _():
+        v_local().wait()
+
+    @pl.when(jnp.logical_not(owner))
+    def _():
+        v_scatter(0, j, 0).wait_recv()
+
+    def v_row(d):
+        return vc.at[rows(256 * j + 32 * ys[d % Y], 32)]
+
+    def v_send(src, slot, d):
+        v_gather[slot] = send(src, src, vg_s.at[slot], vg_r.at[slot], y_peer(d))
+
+    v_gather = {}
+    for d in (2, 6, 1, 7):
+        v_send(v_row(0), d, d)
     totals, t_moves = [], []
     for lc in range(2):
         total = own_part(lc, 0)
@@ -191,10 +222,45 @@
         t_moves.append(send(
             pct.at[lc, own], prt.at[lc, t_z, t_x], one_s.at[2 + lc], one_r.at[2 + lc], t_target
         ))
-    for copy in v_moves:
-        copy.wait_recv()
+    v_gather[2].wait_recv()
+    v_send(v_row(-2), 3, 1)
+    v_send(v_row(-2), 4, 2)
+    v_gather[6].wait_recv()
+    v_send(v_row(2), 5, 7)
+    def x_send(d, lc):
+        part = prt.at[lc, zs[d], x]
+        return [
+            send(part, part, x_s.at[side, lc, d], x_r.at[side, lc, d], x_peer(1 - 2 * side))
+            for side in range(2)
+        ]
+
+    near = (2, 6, 1, 7, 3, 5, 4)
+
+    def z_take(d, lc):
+        z_gather[lc][d].wait_recv()
+        for origin, later, hop in ((2, 3, 1), (2, 4, 2), (6, 5, 7)):
+            if d == origin:
+                part = prt.at[lc, zs[d], x]
+                z_gather[lc][later] = send(
+                    part, part, z_s.at[lc, later], z_r.at[lc, later], z_peer(hop)
+                )
+        x_gather[lc][d] = x_send(d, lc)
+
+    z_gather, x_gather = [], [{}, {}]
+    def z_start(lc):
+        t_moves[lc].wait_recv()
+        chunk = prt.at[lc, z, x]
+        z_gather.append({
+            d: send(chunk, chunk, z_s.at[lc, d], z_r.at[lc, d], z_peer(d)) for d in (2, 6, 1, 7)
+        })
+        x_gather[lc][0] = x_send(0, lc)
+
+    z_start(0)
+    for d in (1, 7, 3, 5, 4):
+        v_gather[d].wait_recv()
     v_half = vc.at[rows(256 * j, 256)]
     v_swap = send(v_half, v_half, one_s.at[4], one_r.at[4], partner)
+    z_start(1)
     v_swap.wait_recv()
     first = vc[0:256, :]
     first = jnp.where(col == 0, unit_lower(first), first)
@@ -210,22 +276,18 @@
         uch[:, 256 * lc : 256 * lc + 256] = high
         ucl[:, 256 * lc : 256 * lc + 256] = low
 
-    def x_send(d, lc):
-        part = prt.at[lc, zs[d], x]
-        return [
-            send(part, part, x_s.at[side, lc, d], x_r.at[side, lc, d], x_peer(1 - 2 * side))
-            for side in range(2)
-        ]
-
-    near = (1, 7, 2, 6, 3, 5, 4)
-    z_gather, x_gather = [], [{}, {}]
-    for lc in range(2):
-        t_moves[lc].wait_recv()
-        chunk = prt.at[lc, z, x]
-        z_gather.append({
-            d: send(chunk, chunk, z_s.at[lc, d], z_r.at[lc, d], z_peer(d)) for d in near
-        })
-        x_gather[lc][0] = x_send(0, lc)
+    forward = [[], []]
+
+    def pass_on(d, lc):
+        x_gather[lc][d][lc].wait_recv()
+        part = prt.at[lc, zs[d], xs[3 - 2 * lc]]
+        forward[lc].append(
+            send(part, part, f_s.at[lc, d], f_r.at[lc, d], x_peer(1 - 2 * lc))
+        )
+
+    for lc in range(2):
+        for d in near[:4]:
+            z_take(d, lc)
     part_sum = gsrc[...]
     for copy, d in zip(g_z, order):
         copy.wait_recv()
@@ -234,19 +296,11 @@
     g_x = [
         send(gsum, gx.at[d], gx_s.at[d], gx_r.at[d], x_peer(d)) for d in range(1, X)
     ]
-
-    forward = [[], []]
-
-    def pass_on(d, lc):
-        x_gather[lc][d][lc].wait_recv()
-        part = prt.at[lc, zs[d], xs[3 - 2 * lc]]
-        forward[lc].append(
-            send(part, part, f_s.at[lc, d], f_r.at[lc, d], x_peer(1 - 2 * lc))
-        )
-
-    for d in near:
-        z_gather[0][d].wait_recv()
-        x_gather[0][d] = x_send(d, 0)
+    for d in (0,) + near[:4]:
+        pass_on(d, 0)
+    for lc in range(2):
+        for d in near[4:]:
+            z_take(d, lc)
     for d, copy in zip(range(1, X), g_x):
         copy.wait_recv()
         part_sum = part_sum + gx[d]
@@ -254,11 +308,8 @@
     g_gather = [
         send(gt.at[own], gt.at[own], y_s.at[1, d], y_r.at[1, d], y_peer(d)) for d in order
     ]
-    for d, e in zip(near, (0,) + near):
-        z_gather[1][d].wait_recv()
-        x_gather[1][d] = x_send(d, 1)
-        pass_on(e, 0)
-    pass_on(near[-1], 0)
+    for d in near[4:]:
+        pass_on(d, 0)
     for d in (0,) + near:
         pass_on(d, 1)
     for copy in p_gather:
@@ -297,6 +348,13 @@
         wl[:, cols] = low
     for copy in started:
         copy.wait_send()
+
+    @pl.when(owner)
+    def _():
+        for d in range(Y):
+            v_scatter(d, 1 - j, 1).wait_send()
+            if d:
+                v_scatter(d, j, 0).wait_send()
 
 
 def finish_kernel(o_ref, uh_ref, ul_ref, wh_ref, wl_ref, out_hbm, buf, sems):
@@ -342,7 +400,7 @@
             vm((512, 256), F32), vm((256, 512), BF16), vm((256, 512), BF16),
             vm((16, 256), F32), vm((8, 16, 256), F32), vm((16, 256), F32),
             vm((4, 16, 256), F32), vm((256, 256), F32),
-            dma((3,)), dma((7,)), dma((7,)), dma((8,)), dma((8,)),
+            dma((3,)), dma((7,)), dma((7,)), dma((8, 2)), dma, dma, dma((8,)), dma((8,)),
             dma((2, 8)), dma((2, 8)), dma((2, 8)), dma((2, 8)),
             dma((2, 8)), dma((2, 8)), dma((8,)), dma((8,)),
             dma((2, 2, 8)), dma((2, 2, 8)), dma((2, 8)), dma((2, 8)), dma((4,)), dma((4,)),

time: 56.9 us -> 55.6 us (0.977)
  Pallas kernels: 56.4 us -> 55.4 us
    pallas_call x1, Pallas kernels: 54.6 us -> 53.6 us  [per_device(): pl.pallas_call(kernel, out_shape=[shape((4096, 128), F32), shape((4, 256,...]
where the time goes in v7:
time: 55.6 us; the launch traced here: 55.4 us
  Pallas kernels  55.4 us (100%)
    pallas_call x1, Pallas kernels, per_device(): pl.pallas_call(kernel, out_shape=[shape((4096, 128), F32), shape((4, 256,...  53.6 us
    pallas_call x1, Pallas kernels, per_device(): pl.pallas_call(finish_kernel, out_shape=shape((4096, 128), F32), in_specs...  1.83 us

profile of v7, /device:TPU:1, one launch (start us, length us, event | category | flops | bytes accessed | tf_op | source)
XLA Modules:
  0.0 55.4 jit_solution(10301517508613224812)
XLA Ops:
  0.0 53.6 %band_update.1 = (f32[4096,128]{1,0:T(8,128)S(1)}, bf16[4,256,256]{2,1,0:T(8,128)(2,1)S(1)}, bf16[4,256,256]{2,1,0:T(8,128)(2,1)S(1)}, bf16[256,512]{1,0:T(8,128)(2,1)S(1)}, bf16[256,512]{1,0:T(8,128)(2,1)S(1)}) custom-call(f32[4096,128]{1,0:T(8,128)} %bitcast.3, f32[4,256,256]{2,1,0:T(8,128)} %bitcast.4, f32[256,256]{1,0:T(8,128)} %t_hbm.1), custom_call_target="tpu_custom_call" | custom-call | tf_op jit(solution)/shard_map/band_update/pallas_call | solution.py:387
  53.6 1.8 %band_finish.1 = f32[4096,128]{1,0:T(8,128)} custom-call(f32[4096,128]{1,0:T(8,128)S(1)} %get-tuple-element.10.o_ref, bf16[4,256,256]{2,1,0:T(8,128)(2,1)S(1)} %get-tuple-element.11.uh_ref, bf16[4,256,256]{2,1,0:T(8,128)(2,1)S(1)} %get-tuple-element.12.ul_ref, bf16[256,512]{1,0:T(8,128)(2,1)S(1)} %get-tuple-element.13.wh_ref, ...), custom_call_target="tpu_custom_call" | custom-call | tf_op jit(solution)/shard_map/band_finish/pallas_call | solution.py:413

commit v8 on v7

--- a/solution.py
+++ b/solution.py
@@ -266,7 +266,9 @@
     first = jnp.where(col == 0, unit_lower(first), first)
     v_cols = [split(first), split(vc[256:512, :])]
     gsrc[...] = dot3(split(totals[0]), v_cols[0], NN) + dot3(split(totals[1]), v_cols[1], NN)
-    g_z = [send(gsrc, gz.at[d], gz_s.at[d], gz_r.at[d], z_peer(d)) for d in order]
+    g_x = [
+        send(gsrc, gx.at[d], gx_s.at[d], gx_r.at[d], x_peer(d)) for d in range(1, X)
+    ]
     p_part = pct.at[:, own]
     p_gather = [
         send(p_part, p_part, y_s.at[0, d], y_r.at[0, d], y_peer(d)) for d in order
@@ -285,25 +287,24 @@
             send(part, part, f_s.at[lc, d], f_r.at[lc, d], x_peer(1 - 2 * lc))
         )
 
-    for lc in range(2):
-        for d in near[:4]:
+    for d in near[:4]:
+        z_take(d, 0)
+    part_sum = gsrc[...]
+    for d, copy in zip(range(1, X), g_x):
+        copy.wait_recv()
+        part_sum = part_sum + gx[d]
+    gsum[...] = part_sum
+    g_z = [send(gsum, gz.at[d], gz_s.at[d], gz_r.at[d], z_peer(d)) for d in order]
+    for d in near[:4]:
+        z_take(d, 1)
+    for d in (0,) + near[:4]:
+        pass_on(d, 0)
+    for lc in range(2):
+        for d in near[4:]:
             z_take(d, lc)
-    part_sum = gsrc[...]
     for copy, d in zip(g_z, order):
         copy.wait_recv()
         part_sum = part_sum + gz[d]
-    gsum[...] = part_sum
-    g_x = [
-        send(gsum, gx.at[d], gx_s.at[d], gx_r.at[d], x_peer(d)) for d in range(1, X)
-    ]
-    for d in (0,) + near[:4]:
-        pass_on(d, 0)
-    for lc in range(2):
-        for d in near[4:]:
-            z_take(d, lc)
-    for d, copy in zip(range(1, X), g_x):
-        copy.wait_recv()
-        part_sum = part_sum + gx[d]
     gt[own, :] = part_sum
     g_gather = [
         send(gt.at[own], gt.at[own], y_s.at[1, d], y_r.at[1, d], y_peer(d)) for d in order

time: 55.6 us -> 57 us (1.025)
  Pallas kernels: 55.4 us -> 56.9 us
    pallas_call x1, Pallas kernels: 53.6 us -> 55 us  [per_device(): pl.pallas_call(kernel, out_shape=[shape((4096, 128), F32), shape((4, 256,...]
where the time goes in v8:
time: 57 us; the launch traced here: 56.9 us
  Pallas kernels  56.9 us (100%)
    pallas_call x1, Pallas kernels, per_device(): pl.pallas_call(kernel, out_shape=[shape((4096, 128), F32), shape((4, 256,...  55 us
    pallas_call x1, Pallas kernels, per_device(): pl.pallas_call(finish_kernel, out_shape=shape((4096, 128), F32), in_specs...  1.83 us

profile of v8, /device:TPU:1, one launch (start us, length us, event | category | flops | bytes accessed | tf_op | source)
XLA Modules:
  0.0 56.9 jit_solution(1656143762302853029)
XLA Ops:
  0.0 55.0 %band_update.1 = (f32[4096,128]{1,0:T(8,128)S(1)}, bf16[4,256,256]{2,1,0:T(8,128)(2,1)S(1)}, bf16[4,256,256]{2,1,0:T(8,128)(2,1)S(1)}, bf16[256,512]{1,0:T(8,128)(2,1)S(1)}, bf16[256,512]{1,0:T(8,128)(2,1)S(1)}) custom-call(f32[4096,128]{1,0:T(8,128)} %bitcast.3, f32[4,256,256]{2,1,0:T(8,128)} %bitcast.4, f32[256,256]{1,0:T(8,128)} %t_hbm.1), custom_call_target="tpu_custom_call" | custom-call | tf_op jit(solution)/shard_map/band_update/pallas_call | solution.py:388
  55.1 1.8 %band_finish.1 = f32[4096,128]{1,0:T(8,128)} custom-call(f32[4096,128]{1,0:T(8,128)S(1)} %get-tuple-element.10.o_ref, bf16[4,256,256]{2,1,0:T(8,128)(2,1)S(1)} %get-tuple-element.11.uh_ref, bf16[4,256,256]{2,1,0:T(8,128)(2,1)S(1)} %get-tuple-element.12.ul_ref, bf16[256,512]{1,0:T(8,128)(2,1)S(1)} %get-tuple-element.13.wh_ref, ...), custom_call_target="tpu_custom_call" | custom-call | tf_op jit(solution)/shard_map/band_finish/pallas_call | solution.py:414

commit v9 on v7

--- a/solution.py
+++ b/solution.py
@@ -120,6 +120,16 @@
         )
 
     loads[0].wait()
+    pl.semaphore_wait(barrier, len(greeted))
+
+    @pl.when(owner)
+    def _():
+        v_local().start()
+        for d in (4, 3, 5, 2, 6, 1, 7, 0):
+            v_scatter(d, 1 - j, 1).start()
+            if d:
+                v_scatter(d, j, 0).start()
+
     for lr in range(4):
         block = v_s[lr]
         if lr == 0:
@@ -148,16 +158,7 @@
     order = (4, 3, 5, 2, 6, 1, 7)
 
     partial(0)
-    pl.semaphore_wait(barrier, len(greeted))
     swaps = [swap_of(0)]
-
-    @pl.when(owner)
-    def _():
-        v_local().start()
-        for d in (4, 3, 5, 2, 6, 1, 7, 0):
-            v_scatter(d, 1 - j, 1).start()
-            if d:
-                v_scatter(d, j, 0).start()
 
     partial(1)
     swaps.append(swap_of(1))
@@ -271,11 +272,6 @@
     p_gather = [
         send(p_part, p_part, y_s.at[0, d], y_r.at[0, d], y_peer(d)) for d in order
     ]
-    for lc in range(2):
-        high, low = split(dot3(factor, v_cols[lc], NT))
-        uch[:, 256 * lc : 256 * lc + 256] = high
-        ucl[:, 256 * lc : 256 * lc + 256] = low
-
     forward = [[], []]
 
     def pass_on(d, lc):
@@ -296,6 +292,10 @@
     g_x = [
         send(gsum, gx.at[d], gx_s.at[d], gx_r.at[d], x_peer(d)) for d in range(1, X)
     ]
+    for lc in range(2):
+        high, low = split(dot3(factor, v_cols[lc], NT))
+        uch[:, 256 * lc : 256 * lc + 256] = high
+        ucl[:, 256 * lc : 256 * lc + 256] = low
     for d in (0,) + near[:4]:
         pass_on(d, 0)
     for lc in range(2):

time: 55.6 us -> 56.6 us (1.018)
  Pallas kernels: 55.4 us -> 56.5 us
    pallas_call x1, Pallas kernels: 53.6 us -> 54.6 us  [per_device(): pl.pallas_call(kernel, out_shape=[shape((4096, 128), F32), shape((4, 256,...]
where the time goes in v9:
time: 56.6 us; the launch traced here: 56.5 us
  Pallas kernels  56.5 us (100%)
    pallas_call x1, Pallas kernels, per_device(): pl.pallas_call(kernel, out_shape=[shape((4096, 128), F32), shape((4, 256,...  54.6 us
    pallas_call x1, Pallas kernels, per_device(): pl.pallas_call(finish_kernel, out_shape=shape((4096, 128), F32), in_specs...  1.83 us

profile of v9, /device:TPU:1, one launch (start us, length us, event | category | flops | bytes accessed | tf_op | source)
XLA Modules:
  0.0 56.5 jit_solution(2629447105677719705)
XLA Ops:
  0.0 54.6 %band_update.1 = (f32[4096,128]{1,0:T(8,128)S(1)}, bf16[4,256,256]{2,1,0:T(8,128)(2,1)S(1)}, bf16[4,256,256]{2,1,0:T(8,128)(2,1)S(1)}, bf16[256,512]{1,0:T(8,128)(2,1)S(1)}, bf16[256,512]{1,0:T(8,128)(2,1)S(1)}) custom-call(f32[4096,128]{1,0:T(8,128)} %bitcast.3, f32[4,256,256]{2,1,0:T(8,128)} %bitcast.4, f32[256,256]{1,0:T(8,128)} %t_hbm.1), custom_call_target="tpu_custom_call" | custom-call | tf_op jit(solution)/shard_map/band_update/pallas_call | solution.py:387
  54.7 1.8 %band_finish.1 = f32[4096,128]{1,0:T(8,128)} custom-call(f32[4096,128]{1,0:T(8,128)S(1)} %get-tuple-element.10.o_ref, bf16[4,256,256]{2,1,0:T(8,128)(2,1)S(1)} %get-tuple-element.11.uh_ref, bf16[4,256,256]{2,1,0:T(8,128)(2,1)S(1)} %get-tuple-element.12.ul_ref, bf16[256,512]{1,0:T(8,128)(2,1)S(1)} %get-tuple-element.13.wh_ref, ...), custom_call_target="tpu_custom_call" | custom-call | tf_op jit(solution)/shard_map/band_finish/pallas_call | solution.py:413
